TPU v7x, 32 devices: a whole 2x2x4 slice. The times are simulated.
32 devices in a mesh: slab: 16 (over z, x, core), col: 2 (over y).
Axes of the slice: x: 2, y: 2, z: 4, core: 2. Of those that a mesh axis runs over, the one named last changes fastest.
Arguments:
- pressure: float32 [1024, 512], P('slab', 'col'), may hold values from 1 to 4
- storage: float32 [1024, 512], P('slab', 'col'), may hold values from 0.5 to 2
- trans: float32 [1024, 512], P('slab', 'col'), may hold values from 0.5 to 8
- source: float32 [1024, 512], P('slab', 'col'), may hold values from -1.2 to 1.2
- shells_old: float32 [2, 1024, 64, 128], P('col', 'slab'), may hold values from 1 to 2
- shell_cap: float32 [64], replicated, may hold values from 0.5 to 4
- shell_trans: float32 [64], replicated, may hold values from 0.5 to 4
- new_source: int32 [2, 512], P('col'), may hold values from 0 to 1023, as said below
- cell_block: int32 [2, 1024], P('col', 'slab'), may hold values from 0 to 127, as said below
Outputs:
- pressure_out: float32 [1024, 512], P('slab', 'col')
- shells_new: float32 [2, 512, 64, 128], P('col', 'slab')
Inputs may be any that keep to these rules, and one draw needn't show every extreme that they name: `new_source`: within each col index, every old slot is taken at most once; the slots after the move on one slab device take blocks from 8 distinct slab devices, exactly 4 blocks from each; the taken old slots lie only on the even-numbered slab devices, each of which has all 64 of its slots taken. `cell_block`: within one slab device and col index the entries are distinct.
All inputs are finite; a program needn't handle non-finite values.
Results may differ from a plain program's by a relative error of at most 0.0003.
Values sent between devices are 32-bit elements; how exact they have to be, the bound alone decides.
No kernel may reach another device: no remote copies, remote signals or barrier semaphores. Data moves between devices by JAX's collectives and lax.ppermute only.
A program may use at most 128 MiB of HBM per device.

v0:
```python
import functools

import jax
import jax.numpy as jnp
from jax import lax
from jax.experimental import pallas as pl
from jax.experimental.pallas import tpu as pltpu
from jax.sharding import PartitionSpec as P


CAP = 4
STEPS = 2
ITERS = 3
EDGE = 8
LANES = 128
FIELDS = 7
GRANT = 16 * 2**20
FILL = (1.0, 1.0, 0.0, 0.0, 0.0, 0.0, 0.0)


VMEM = pl.BlockSpec(memory_space=pltpu.VMEM)
SMEM = pl.BlockSpec(memory_space=pltpu.SMEM)
ANY = pl.BlockSpec(memory_space=pl.ANY)
HBM = pl.BlockSpec(memory_space=pltpu.HBM)


def iota(shape, dim):
    return lax.broadcasted_iota(jnp.int32, shape, dim)


def split_by(value, size):
    if size & (size - 1) == 0:
        return value >> (size.bit_length() - 1), value & (size - 1)
    return value // size, value % size


def column_of(row, eye):
    return jnp.sum(jnp.where(eye, row, 0.0), axis=1, keepdims=True)


def row_of(column, count):
    eye = iota((count, count), 0) == iota((count, count), 1)
    return jnp.sum(jnp.where(eye, column, 0.0), axis=0, keepdims=True)


def placed(target, value, count):
    width = target.shape[1]
    hit = iota((count, width), 0) == target
    column = jnp.sum(jnp.where(hit, value.astype(jnp.float32), 0.0), axis=1, keepdims=True)
    return row_of(column, count).astype(jnp.int32)


def inverse_of(cap_row, trans_row):
    count = cap_row.shape[1]
    rows, cols = iota((count, count), 0), iota((count, count), 1)
    eye = rows == cols
    cap = column_of(cap_row, eye)
    trans = column_of(trans_row, eye)
    above = column_of(trans_row, cols == rows + 1)
    shape = (count, LANES)
    diag = jnp.broadcast_to(cap + trans + above, shape)
    low = jnp.broadcast_to(jnp.where(iota((count, 1), 0) == 0, 0.0, trans), shape)
    high = jnp.broadcast_to(above, shape)
    rhs = jnp.where(iota(shape, 0) == iota(shape, 1), 1.0, 0.0)
    step = 1
    while step < count:
        down = functools.partial(pltpu.roll, shift=step, axis=0)
        up = functools.partial(pltpu.roll, shift=count - step, axis=0)
        alpha = low / down(diag)
        gamma = high / up(diag)
        diag = diag - alpha * down(high) - gamma * up(low)
        rhs = rhs + alpha * down(rhs) + gamma * up(rhs)
        low, high = alpha * down(low), gamma * up(high)
        step *= 2
    return rhs / diag, cap, trans


def pack_sides(get, rows):
    lane = iota((rows, LANES), 1)
    out = jnp.zeros((rows, LANES), jnp.float32)
    for f in range(FIELDS):
        value = get(f)
        first, last = value[:, :LANES], value[:, -LANES:]
        at = 2 * EDGE * f
        moved = pltpu.roll(first, at, axis=1) if at else first
        out = jnp.where((lane >= at) & (lane < at + EDGE), moved, out)
        moved = pltpu.roll(last, (at + 2 * EDGE) % LANES, axis=1)
        out = jnp.where((lane >= at + EDGE) & (lane < at + 2 * EDGE), moved, out)
    return out


def base_kernel(
    cap_hbm, trans_hbm, table_hbm, block_hbm, shells_hbm, p_hbm, storage_hbm, t_hbm, source_hbm,
    inv_ref, const_ref, slot_ref, place_ref, recv_ref, cap_ref, trans_ref, held,
    p_ref, storage_ref, t_ref, source_ref, b1_ref, b2_ref, e_ref, a_ref, b_ref, side_ref,
    tiles, table_ref, block_row, block_ref, sem, chunk_sem,
):
    me = lax.axis_index("slab")
    slabs = lax.axis_size("slab")
    even = me % 2 == 0
    old_slots, count, _ = shells_hbm.shape
    chunks = 4
    per = old_slots // chunks
    loads = [
        pltpu.make_async_copy(source, target, sem.at[i])
        for i, (source, target) in enumerate((
            (cap_hbm, cap_ref), (trans_hbm, trans_ref), (p_hbm, p_ref), (storage_hbm, storage_ref),
            (t_hbm, t_ref), (source_hbm, source_ref), (table_hbm, table_ref),
            (block_hbm, block_row), (block_hbm, block_ref),
        ))
    ]
    for load in loads:
        load.start()

    def chunk(i):
        part = pl.ds(i * per, per)
        return pltpu.make_async_copy(shells_hbm.at[part], held.at[part], chunk_sem.at[i])

    @pl.when(even)
    def _():
        for i in range(chunks):
            chunk(i).start()

    for load in loads:
        load.wait()
    cap_row, trans_row = cap_ref[...], trans_ref[...]
    inverse, cap, _ = inverse_of(cap_row, trans_row)
    inv_ref[...] = inverse
    t0 = trans_row[:, 0:1]
    first_row = inverse[0:1, :count] * cap_row
    w1 = inverse[:, 0:1] * cap
    w2 = cap * jnp.sum(inverse[:, :count] * first_row, axis=1, keepdims=True)
    couple_row = inverse[0:1, :count] * t0
    c0 = couple_row[:, 0:1]
    c1 = jnp.sum(first_row * couple_row, axis=1, keepdims=True)
    coupling = t0 * (1.0 - c0)
    const_ref[...] = jnp.broadcast_to(t0 * c1 / coupling, const_ref.shape)

    tiles[...] = jnp.zeros_like(tiles)

    @pl.when(even)
    def _():
        v1 = jnp.broadcast_to(t0 * w1, (count, LANES))
        v2 = jnp.broadcast_to(t0 * w2, (count, LANES))
        on = jnp.broadcast_to(coupling, (1, LANES))
        per_row = p_ref.shape[1] // LANES
        for i in range(chunks):
            chunk(i).wait()

            def body(j, carry):
                for u in range(4):
                    slot = i * per + j * 4 + u
                    data = held[slot]
                    row, half = split_by(block_ref[0, slot], per_row)
                    at = pl.ds(row, 1)
                    tiles[0, half, at] = jnp.sum(v1 * data, axis=0, keepdims=True)
                    tiles[1, half, at] = jnp.sum(v2 * data, axis=0, keepdims=True)
                    tiles[2, half, at] = on
                return carry

            lax.fori_loop(0, per // 4, body, 0)

    for i, ref in enumerate((b1_ref, b2_ref, e_ref)):
        ref[...] = jnp.concatenate([tiles[i, h] for h in range(tiles.shape[1])], axis=1)
    fields = (p_ref, storage_ref, t_ref, source_ref, b1_ref, b2_ref, e_ref)
    height = p_ref.shape[0]
    for f, ref in enumerate(fields):
        top, bottom = ref[0:EDGE, :], ref[height - EDGE : height, :]
        a_ref[f] = jnp.where(even, bottom, top)
        b_ref[f] = jnp.where(even, top, bottom)
    side_ref[...] = pack_sides(lambda f: fields[f][...], height)

    table = table_ref[...]
    total = table.shape[1]
    new_slots = total // slabs
    anchor, local = split_by(table, old_slots)
    lane = iota((1, total), 1)
    dest, within = split_by(lane, new_slots)
    rank = jnp.zeros((1, total), jnp.int32)
    for shift in range(1, new_slots):
        same = (pltpu.roll(anchor, shift, axis=1) == anchor) & (within >= shift)
        rank = rank + jnp.where(same, 1, 0)
    rank = jnp.minimum(rank, CAP - 1)
    mine = anchor == me - me % 2
    target = jnp.where(mine, dest * CAP + rank, -1)
    slot_ref[...] = placed(target, local, slabs * CAP)
    eye = iota((old_slots, old_slots), 0) == iota((old_slots, old_slots), 1)
    column = column_of(block_row[...].astype(jnp.float32), eye)
    owner = iota((old_slots, total), 0) == local
    here = jnp.sum(jnp.where(owner, column, 0.0), axis=0, keepdims=True)
    place_ref[...] = placed(target, here, slabs * CAP)
    recv = ((anchor >> 1) ^ (me // 2)) * CAP + rank
    recv_ref[...] = placed(lane - me * new_slots, recv, new_slots)


def pack_kernel(slot_ref, own_ref, other_ref, *out_refs):
    me = lax.axis_index("slab")
    chip, core = me // 2, me % 2
    count = own_ref.shape[1]

    def fill(source):
        for k, ref in enumerate(out_refs):
            for r in range(CAP):
                ref[r, :count] = source[slot_ref[0, ((chip ^ k) * 2 + core) * CAP + r]]

    @pl.when(core == 0)
    def _():
        fill(own_ref)

    @pl.when(core == 1)
    def _():
        fill(other_ref)


def rows_kernel(own_ref, other_ref, *rest):
    near = [ref for ref in rest if len(ref.shape) == 3]
    rest = rest[len(near) // 2 :]
    near, (local, *far) = near[len(near) // 2 :], [ref for ref in rest if len(ref.shape) == 2]
    me = lax.axis_index("slab")
    chip, core = me // 2, me % 2
    for k in range(len(near) + len(far) + 1):
        at = (chip ^ k) * 2 + core
        rows = jnp.where(core == 0, own_ref[at], other_ref[at])
        if k == 0:
            local[...] = rows
        elif k <= len(near):
            ref = near[k - 1]
            ref[0, ref.shape[1] - rows.shape[0] :] = rows
        else:
            far[k - len(near) - 1][...] = rows


def side_kernel(side_ref, a_ref, b_ref, out_ref):
    even = lax.axis_index("slab") % 2 == 0
    height = side_ref.shape[0]
    from_a = pack_sides(lambda f: a_ref[f], EDGE)
    from_b = pack_sides(lambda f: b_ref[f], EDGE)
    out_ref[0:EDGE] = jnp.where(even, from_b, from_a)
    out_ref[EDGE : EDGE + height] = side_ref[...]
    out_ref[EDGE + height :] = jnp.where(even, from_a, from_b)


def fracture_kernel(
    place_ref, const_ref, p_ref, storage_ref, t_ref, source_ref, b1_ref, b2_ref, e_ref,
    a_ref, b_ref, c_ref, d_ref, out_ref, rows_ref, keep,
):
    me, slabs = lax.axis_index("slab"), lax.axis_size("slab")
    col, cols = lax.axis_index("col"), lax.axis_size("col")
    even, col_even = me % 2 == 0, col % 2 == 0
    height, width = p_ref.shape
    tall, wide = height + 2 * EDGE, width + LANES
    row, lane = iota((tall, wide), 0), iota((tall, wide), 1)
    missing = (
        ((me == 0) & (row < EDGE))
        | ((me == slabs - 1) & (row >= EDGE + height))
        | ((lane >= width) & (lane < wide - EDGE) & ((lane >= width + EDGE) | (col == cols - 1)))
        | ((lane >= wide - EDGE) & (col == 0))
    )
    side_lane = iota((tall, LANES), 1)
    right = jnp.where(col_even, c_ref[...], d_ref[...])
    left = jnp.where(col_even, d_ref[...], c_ref[...])
    refs = (p_ref, storage_ref, t_ref, source_ref, b1_ref, b2_ref, e_ref)

    def extended(f):
        top = jnp.where(even, b_ref[f], a_ref[f])
        bottom = jnp.where(even, a_ref[f], b_ref[f])
        own = jnp.concatenate([top, refs[f][...], bottom], axis=0)
        at = 2 * EDGE * f
        from_right = pltpu.roll(right, LANES - at, axis=1) if at else right
        from_left = pltpu.roll(left, LANES - 2 * EDGE - at, axis=1)
        side = jnp.where(side_lane < EDGE, from_right, from_left)
        return jnp.where(missing, FILL[f], jnp.concatenate([own, side], axis=1))

    p, storage, t, source, base1, base2, coef = (extended(f) for f in range(FIELDS))
    next_lane = functools.partial(pltpu.roll, shift=wide - 1, axis=1)
    prev_lane = functools.partial(pltpu.roll, shift=1, axis=1)
    next_row = functools.partial(pltpu.roll, shift=tall - 1, axis=0)
    prev_row = functools.partial(pltpu.roll, shift=1, axis=0)

    def face_of(near):
        total = t + near
        return jnp.where(total > 0.0, 2.0 * t * near / jnp.where(total > 0.0, total, 1.0), 0.0)

    face_h, face_v = face_of(next_lane(t)), face_of(next_row(t))
    conduct = face_h + prev_lane(face_h) + face_v + prev_row(face_v)
    half_h, half_v = face_h * 0.5, face_v * 0.5
    fixed = storage + coef
    rhs = source + base1
    ratio = const_ref[0:1, 0:1]
    for step in range(STEPS):
        prev = p
        for sweep in range(ITERS):
            if sweep == ITERS - 1:
                mid = p[EDGE : EDGE + height]
                for h in range(width // LANES):
                    keep[step, h] = mid[:, h * LANES : (h + 1) * LANES]
                last = p
            near = next_lane(p)
            flow_h = half_h * (near + p) * (near - p)
            near = next_row(p)
            flow_v = half_v * (near + p) * (near - p)
            flux = flow_h - prev_lane(flow_h) + flow_v - prev_row(flow_v)
            misfit = storage * (p - prev) - flux + coef * p - rhs
            p = p - misfit / (fixed + p * conduct)
        rhs = source + base2 + ratio * coef * last
    out_ref[...] = p[EDGE : EDGE + height, :width]

    def body(d, carry):
        for r in range(CAP):
            at_row, half = split_by(place_ref[0, d * CAP + r], width // LANES)
            for step in range(STEPS):
                rows_ref[d, pl.ds(step * CAP + r, 1)] = keep[step, half, pl.ds(at_row, 1)]
        return carry

    lax.fori_loop(0, slabs, body, 0)


def final_kernel(recv_ref, cap_ref, trans_ref, inv_ref, *rest):
    *in_refs, out_ref, held, rows, done, sem = rest
    slots, count = out_ref.shape[:2]
    blocks = [ref for ref in in_refs if len(ref.shape) == 3]
    loose = [ref for ref in in_refs if len(ref.shape) == 2]
    for k, ref in enumerate(blocks):
        held[pl.ds(k * CAP, CAP)] = ref[:, :count]
        inside = ref.shape[1] > count
        rows[k] = ref[0, count:] if inside else loose.pop(0)[...]
    cap_row = cap_ref[...]
    inverse = inv_ref[:, :count]
    t0 = trans_ref[:, 0:1]
    a = inverse * cap_row
    couple = inv_ref[:, 0:1] * t0
    couple2 = jnp.sum(a * (inverse[0:1, :] * t0), axis=1, keepdims=True)
    square = jnp.dot(a, a, preferred_element_type=jnp.float32, precision=lax.Precision.HIGHEST)
    high = square.astype(jnp.bfloat16)
    low = (square - high.astype(jnp.float32)).astype(jnp.bfloat16)
    left = jnp.concatenate([high, high, low], axis=1)
    m1 = jnp.broadcast_to(couple2, (count, LANES))
    m2 = jnp.broadcast_to(couple, (count, LANES))
    pair = 2

    def write(j):
        part = pl.ds(j * pair, pair)
        return pltpu.make_async_copy(done.at[part], out_ref.at[part], sem.at[j])

    for j in range(slots // pair):
        parts = []
        for u in range(pair):
            data = held[recv_ref[0, j * pair + u]]
            hi = data.astype(jnp.bfloat16)
            lo = (data - hi.astype(jnp.float32)).astype(jnp.bfloat16)
            parts.append(jnp.concatenate([hi, lo, hi], axis=0))
        product = jnp.dot(left, jnp.concatenate(parts, axis=1), preferred_element_type=jnp.float32)
        for u in range(pair):
            k, r = split_by(recv_ref[0, j * pair + u], CAP)
            p1 = rows[k, pl.ds(r, 1)]
            p2 = rows[k, pl.ds(r + CAP, 1)]
            done[j * pair + u] = product[:, u * LANES : (u + 1) * LANES] + m1 * p1 + m2 * p2
        write(j).start()
    for j in range(slots // pair):
        write(j).wait()


def call(kernel, out_shape, in_specs, out_specs, args, scratch=(), aliases=None):
    return pl.pallas_call(
        kernel,
        out_shape=out_shape,
        in_specs=in_specs,
        out_specs=out_specs,
        scratch_shapes=scratch,
        input_output_aliases=aliases or {},
        compiler_params=pltpu.CompilerParams(vmem_limit_bytes=GRANT),
    )(*args)


def f32(*shape):
    return jax.ShapeDtypeStruct(shape, jnp.float32)


def i32(*shape):
    return jax.ShapeDtypeStruct(shape, jnp.int32)


def swaps(size, odd):
    if not odd:
        return [(i, i ^ 1) for i in range(size)]
    return [(i, min(max(((i + 1) ^ 1) - 1, 0), size - 1)) for i in range(size)]


def distances(slabs):
    chips = slabs // 2
    return list(range(1, chips // 2)), list(range(chips // 2, chips))


def shards(
    pressure, storage, trans, source, shells_old, shell_cap, shell_trans, new_source, cell_block
):
    slabs, cols = lax.axis_size("slab"), lax.axis_size("col")
    height, width = pressure.shape
    old_slots, count, cells = shells_old.shape[1:]
    new_slots = new_source.shape[1] // slabs
    chips = slabs // 2
    shells = shells_old[0]
    cap_row, trans_row = shell_cap.reshape(1, count), shell_trans.reshape(1, count)

    tall = height + 2 * EDGE
    tail = STEPS * CAP
    near_k, far_k = distances(slabs)

    def chip_swap(value, k):
        return lax.ppermute(value, "slab", [(i, i ^ (2 * k)) for i in range(slabs)])

    hopped = lax.ppermute(shells, "slab", swaps(slabs, False))
    plane, edge = f32(height, width), f32(FIELDS, EDGE, width)
    (
        inverse, const, slot, place, recv, cap_row, trans_row, held,
        pressure, storage, trans, source, base1, base2, coef, edge_a, edge_b, side,
    ) = call(
        base_kernel,
        (
            f32(count, LANES), f32(1, LANES), i32(1, slabs * CAP), i32(1, slabs * CAP),
            i32(1, new_slots), f32(1, count), f32(1, count), f32(old_slots, count, cells),
            *(plane,) * 7, edge, edge, f32(height, LANES),
        ),
        [HBM] * 9,
        (VMEM,) * 18,
        tuple(
            pltpu.with_memory_space_constraint(value, pltpu.HBM)
            for value in (
                cap_row, trans_row, new_source, cell_block, shells, pressure, storage, trans, source
            )
        ),
        [
            pltpu.VMEM((3, width // LANES, height, LANES), jnp.float32),
            pltpu.VMEM(new_source.shape, jnp.int32),
            pltpu.VMEM(cell_block.shape, jnp.int32),
            pltpu.SMEM(cell_block.shape, jnp.int32),
            pltpu.SemaphoreType.DMA((9,)),
            pltpu.SemaphoreType.DMA((4,)),
        ],
    )
    edge_b = lax.ppermute(edge_b, "slab", swaps(slabs, True))
    edge_a = lax.ppermute(edge_a, "slab", swaps(slabs, False))
    packed = call(
        pack_kernel,
        tuple(f32(CAP, count + (tail if k in near_k else 0), cells) for k in range(chips)),
        [SMEM, VMEM, VMEM],
        (VMEM,) * chips,
        (slot, held, hopped),
    )
    side = call(side_kernel, f32(tall, LANES), [VMEM] * 3, VMEM, (side, edge_a, edge_b))
    side_c = lax.ppermute(side, "col", swaps(cols, False))
    side_d = lax.ppermute(side, "col", swaps(cols, True)) if cols > 2 else side_c
    far = [chip_swap(packed[k], k) for k in far_k]

    result, rows = call(
        fracture_kernel,
        (plane, f32(slabs, tail, LANES)),
        [SMEM] + [VMEM] * 12,
        (VMEM, VMEM),
        (
            place, const, pressure, storage, trans, source, base1, base2, coef,
            edge_a, edge_b, side_c, side_d,
        ),
        [pltpu.VMEM((STEPS, width // LANES, height, LANES), jnp.float32)],
    )
    other_rows = lax.ppermute(rows, "slab", swaps(slabs, False))
    filled = call(
        rows_kernel,
        tuple(f32(CAP, count + tail, cells) for k in near_k) + (f32(tail, cells),) * (1 + len(far_k)),
        [VMEM] * (2 + len(near_k)),
        (VMEM,) * chips,
        (rows, other_rows, *(packed[k] for k in near_k)),
        aliases={2 + i: i for i in range(len(near_k))},
    )
    near, (local_rows, *far_rows) = filled[: len(near_k)], filled[len(near_k) :]
    near = [chip_swap(value, k) for value, k in zip(near, near_k)]
    far_rows = [chip_swap(value, k) for value, k in zip(far_rows, far_k)]
    shells_new = call(
        final_kernel,
        f32(new_slots, count, cells),
        [SMEM] + [VMEM] * (3 + chips + 1 + len(far_k)),
        ANY,
        (recv, cap_row, trans_row, inverse, packed[0], *near, *far, local_rows, *far_rows),
        [
            pltpu.VMEM((chips * CAP, count, cells), jnp.float32),
            pltpu.VMEM((chips, tail, cells), jnp.float32),
            pltpu.VMEM((new_slots, count, cells), jnp.float32),
            pltpu.SemaphoreType.DMA((new_slots // 2,)),
        ],
    )
    return (result, shells_new[None])


def solution(mesh):
    placed_at = (
        P("slab", "col"),
        P("slab", "col"),
        P("slab", "col"),
        P("slab", "col"),
        P("col", "slab", None, None),
        P(),
        P(),
        P("col", None),
        P("col", "slab"),
    )
    return jax.shard_map(
        shards,
        mesh=mesh,
        in_specs=placed_at,
        out_specs=(P("slab", "col"), P("col", "slab", None, None)),
        check_vma=False,
    )
```

profile of v0, /device:TPU:16, one launch (start us, length us, event | category | flops | bytes accessed | tf_op | source)
XLA Modules:
  0.0 51.0 jit_solution(1397644234435694542)
XLA Ops:
  0.6 0.1 collective-permute-start.3
  0.7 3.3 %shard_map.104 = (f32[64,128]{1,0:T(8,128)S(1)}, f32[1,128]{1,0:T(1,128)S(1)}, s32[1,64]{1,0:T(1,128)S(1)}, s32[1,64]{1,0:T(1,128)S(1)}, s32[1,32]{1,0:T(1,128)S...) custom-call(f32[1,64]{1,0:T(1,128)} %bitcast.7, ...), custom_call_target="tpu_custom_call" | custom-call | tf_op jit(solution)/shard_map/pallas_call | solution.py:364
  4.0 0.1 collective-permute-start
  4.1 3.4 %collective-permute-start.1 = (f32[7,8,256]{2,1,0:T(8,128)S(1)}, f32[7,8,256]{2,1,0:T(8,128)S(1)}, u32[]{:S(2)}, u32[]{:S(2)}) collective-permute-start(f32[7,8,256]{2,1,0:T(8,128)S(1)} %get-tuple-element.48), channel_id=1, source_target_pairs={{0,0},{2,4},{4,2},{6,8},{8,6},{10,12},{12,10},{14,16},{16,14},{18,... | collective-permute-start | bytes 172040 | tf_op jit(solution)/shard_map/ppermute | solution.py:441
  7.4 0.0 collective-permute-done.a_ref
  7.4 3.1 %collective-permute-done.1.b_ref = f32[7,8,256]{2,1,0:T(8,128)S(1)} collective-permute-done((f32[7,8,256]{2,1,0:T(8,128)S(1)}, f32[7,8,256]{2,1,0:T(8,128)S(1)}, u32[]{:S(2)}, u32[]{:S(2)}) %collective-permute-start.1) | collective-permute-done | bytes 57376 | tf_op jit(solution)/shard_map/ppermute | solution.py:441
  10.5 0.1 shard_map.105
  10.6 1.6 %collective-permute-start.2 = (f32[80,128]{1,0:T(8,128)S(1)}, f32[80,128]{1,0:T(8,128)S(1)}, u32[]{:S(2)}, u32[]{:S(2)}) collective-permute-start(f32[80,128]{1,0:T(8,128)S(1)} %shard_map.105), channel_id=1, source_target_pairs={{0,1},{1,0},{2,3},{3,2},{4,5},{5,4},{6,7},{7,6},{8,9},{9,8},{10,11... | collective-permute-start | bytes 122888 | tf_op jit(solution)/shard_map/ppermute | solution.py:451
  12.2 0.0 collective-permute-done.3.other_ref
  12.2 0.6 %shard_map.107 = (f32[4,64,128]{2,1,0:T(8,128)S(1)}, f32[4,72,128]{2,1,0:T(8,128)S(1)}, f32[4,72,128]{2,1,0:T(8,128)S(1)}, f32[4,72,128]{2,1,0:T(8,128)S(1)}, f3...) custom-call(s32[1,64]{1,0:T(1,128)S(1)} %get-tuple-element.55.slot_r, ...), custom_call_target="tpu_custom_call" | custom-call | tf_op jit(solution)/shard_map/pallas_call | solution.py:364
  12.9 0.1 collective-permute-start.8
  13.0 2.8 %collective-permute-start.9 = (f32[4,64,128]{2,1,0:T(8,128)S(1)}, f32[4,64,128]{2,1,0:T(8,128)S(1)}, u32[]{:S(2)}, u32[]{:S(2)}) collective-permute-start(f32[4,64,128]{2,1,0:T(8,128)S(1)} %get-tuple-element.66), channel_id=1, source_target_pairs={{0,20},{2,22},{4,16},{6,18},{8,28},{10,30},{12,24},{14,26},{16,4},... | collective-permute-start | bytes 393224 | tf_op jit(solution)/shard_map/ppermute | solution.py:410
  15.8 0.0 collective-permute-done.2.c_ref.d_ref
  15.8 2.7 %shard_map.106 = (f32[64,256]{1,0:T(8,128)}, f32[16,8,128]{2,1,0:T(8,128)S(1)}) custom-call(s32[1,64]{1,0:T(1,128)S(1)} %get-tuple-element.38.place_ref, f32[1,128]{1,0:T(1,128)S(1)} %get-tuple-element.39.const_ref, f32[64,256]{1,0:T(8,128)S(1)} %get-tuple-element.40.p_ref, f32[64,256]{1,0:T(8,128)S(1)} %get-tuple-element.41.storage_ref, ...), custom_call_target="tpu_custom_call" | custom-call | tf_op jit(solution)/shard_map/pallas_call | solution.py:364
  18.5 0.5 %collective-permute-start.4 = (f32[16,8,128]{2,1,0:T(8,128)S(1)}, f32[16,8,128]{2,1,0:T(8,128)S(1)}, u32[]{:S(2)}, u32[]{:S(2)}) collective-permute-start(f32[16,8,128]{2,1,0:T(8,128)S(1)} %get-tuple-element.58.own_ref), channel_id=1, source_target_pairs={{0,2},{2,0},{4,6},{6,4},{8,10},{10,8},{12,14},{14,12},{16,18},{18,... | collective-permute-start | bytes 196616 | tf_op jit(solution)/shard_map/ppermute | solution.py:466
  19.1 0.9 %collective-permute-done.4.other_ref = f32[16,8,128]{2,1,0:T(8,128)S(1)} collective-permute-done((f32[16,8,128]{2,1,0:T(8,128)S(1)}, f32[16,8,128]{2,1,0:T(8,128)S(1)}, u32[]{:S(2)}, u32[]{:S(2)}) %collective-permute-start.4) | collective-permute-done | bytes 65568 | tf_op jit(solution)/shard_map/ppermute | solution.py:466
  20.0 0.4 collective-permute-start.12
  20.4 3.3 %collective-permute-start.13 = (f32[8,128]{1,0:T(8,128)S(1)}, f32[8,128]{1,0:T(8,128)S(1)}, u32[]{:S(2)}, u32[]{:S(2)}) collective-permute-start(f32[8,128]{1,0:T(8,128)S(1)} %get-tuple-element.71), channel_id=1, source_target_pairs={{0,20},{2,22},{4,16},{6,18},{8,28},{10,30},{12,24},{14,26},{16,4},... | collective-permute-start | bytes 12296 | tf_op jit(solution)/shard_map/ppermute | solution.py:410
  23.7 0.4 collective-permute-start.14
  24.2 0.5 collective-permute-done.12.rest_9_
  24.7 2.4 %collective-permute-start.15 = (f32[8,128]{1,0:T(8,128)S(1)}, f32[8,128]{1,0:T(8,128)S(1)}, u32[]{:S(2)}, u32[]{:S(2)}) collective-permute-start(f32[8,128]{1,0:T(8,128)S(1)} %get-tuple-element.73), channel_id=1, source_target_pairs={{0,28},{2,30},{4,24},{6,26},{8,20},{10,22},{12,16},{14,18},{16,12}... | collective-permute-start | bytes 12296 | tf_op jit(solution)/shard_map/ppermute | solution.py:410
  27.1 0.0 collective-permute-done.13.rest_10_
  27.1 1.8 %collective-permute-start.5 = (f32[4,72,128]{2,1,0:T(8,128)S(1)}, f32[4,72,128]{2,1,0:T(8,128)S(1)}, u32[]{:S(2)}, u32[]{:S(2)}) collective-permute-start(f32[4,72,128]{2,1,0:T(8,128)S(1)} %get-tuple-element.62), channel_id=1, source_target_pairs={{0,4},{2,6},{4,0},{6,2},{8,12},{10,14},{12,8},{14,10},{16,20},{18,... | collective-permute-start | bytes 442376 | tf_op jit(solution)/shard_map/ppermute | solution.py:410
  28.9 0.0 collective-permute-done.14.rest_11_
  28.9 2.1 %collective-permute-start.6 = (f32[4,72,128]{2,1,0:T(8,128)S(1)}, f32[4,72,128]{2,1,0:T(8,128)S(1)}, u32[]{:S(2)}, u32[]{:S(2)}) collective-permute-start(f32[4,72,128]{2,1,0:T(8,128)S(1)} %get-tuple-element.63), channel_id=1, source_target_pairs={{0,8},{2,10},{4,12},{6,14},{8,0},{10,2},{12,4},{14,6},{16,24},{18,... | collective-permute-start | bytes 442376 | tf_op jit(solution)/shard_map/ppermute | solution.py:410
  31.0 0.0 collective-permute-done.15.rest_12_
  31.0 4.5 %collective-permute-start.7 = (f32[4,72,128]{2,1,0:T(8,128)S(1)}, f32[4,72,128]{2,1,0:T(8,128)S(1)}, u32[]{:S(2)}, u32[]{:S(2)}) collective-permute-start(f32[4,72,128]{2,1,0:T(8,128)S(1)} %get-tuple-element.64), channel_id=1, source_target_pairs={{0,12},{2,14},{4,8},{6,10},{8,4},{10,6},{12,0},{14,2},{16,28},{18,... | collective-permute-start | bytes 442376 | tf_op jit(solution)/shard_map/ppermute | solution.py:410
  35.4 0.0 collective-permute-done.8.rest_4_
  35.4 0.5 %collective-permute-start.10 = (f32[4,64,128]{2,1,0:T(8,128)S(1)}, f32[4,64,128]{2,1,0:T(8,128)S(1)}, u32[]{:S(2)}, u32[]{:S(2)}) collective-permute-start(f32[4,64,128]{2,1,0:T(8,128)S(1)} %get-tuple-element.67), channel_id=1, source_target_pairs={{0,24},{2,26},{4,28},{6,30},{8,16},{10,18},{12,20},{14,22},{16,8},... | collective-permute-start | bytes 393224 | tf_op jit(solution)/shard_map/ppermute | solution.py:410
  35.9 0.0 collective-permute-done.9.rest_5_
  35.9 2.6 %collective-permute-start.11 = (f32[4,64,128]{2,1,0:T(8,128)S(1)}, f32[4,64,128]{2,1,0:T(8,128)S(1)}, u32[]{:S(2)}, u32[]{:S(2)}) collective-permute-start(f32[4,64,128]{2,1,0:T(8,128)S(1)} %get-tuple-element.68), channel_id=1, source_target_pairs={{0,28},{2,30},{4,24},{6,26},{8,20},{10,22},{12,16},{14,18},{16,12}... | collective-permute-start | bytes 393224 | tf_op jit(solution)/shard_map/ppermute | solution.py:410
  38.6 7.6 %collective-permute-done.10.rest_6_ = f32[4,64,128]{2,1,0:T(8,128)S(1)} collective-permute-done((f32[4,64,128]{2,1,0:T(8,128)S(1)}, f32[4,64,128]{2,1,0:T(8,128)S(1)}, u32[]{:S(2)}, u32[]{:S(2)}) %collective-permute-start.10) | collective-permute-done | bytes 131104 | tf_op jit(solution)/shard_map/ppermute | solution.py:410
  46.2 2.7 %collective-permute-done.11.rest_7_ = f32[4,64,128]{2,1,0:T(8,128)S(1)} collective-permute-done((f32[4,64,128]{2,1,0:T(8,128)S(1)}, f32[4,64,128]{2,1,0:T(8,128)S(1)}, u32[]{:S(2)}, u32[]{:S(2)}) %collective-permute-start.11) | collective-permute-done | bytes 131104 | tf_op jit(solution)/shard_map/ppermute | solution.py:410
  48.9 0.0 collective-permute-done.5.rest_1_
  48.9 0.0 collective-permute-done.6.rest_2_
  48.9 0.0 collective-permute-done.7.rest_3_
  48.9 2.1 %shard_map.109 = f32[32,64,128]{2,1,0:T(8,128)} custom-call(s32[1,32]{1,0:T(1,128)S(1)} %get-tuple-element.51.recv_ref, f32[1,64]{1,0:T(1,128)S(1)} %get-tuple-element.52.cap_ref, f32[1,64]{1,0:T(1,128)S(1)} %get-tuple-element.53.trans_ref, f32[64,128]{1,0:T(8,128)S(1)} %get-tuple-element.54.inv_ref, f32[4,64,128]{2,1,0:T(8,128)S(1)} %get-tuple-element.57.rest_0_, ...), custom_call_target="tpu_custom_call" | custom-call | tf_op jit(solution)/shard_map/pallas_call | solution.py:364
  (1 shorter events, 0.0 us)
Async XLA Ops:
  0.6 11.6 %collective-permute-start.3 = (f32[64,64,128]{2,1,0:T(8,128)}, f32[64,64,128]{2,1,0:T(8,128)S(1)}, u32[]{:S(2)}, u32[]{:S(2)}) collective-permute-start(f32[64,64,128]{2,1,0:T(8,128)} %bitcast.4), channel_id=1, source_target_pairs={{0,2},{2,0},{4,6},{6,4},{8,10},{10,8},{12,14},{14,12},{16,18},{18,... | collective-permute-start | bytes 6291464 | tf_op jit(solution)/shard_map/ppermute | solution.py:412
  4.0 3.5 %collective-permute-start = (f32[7,8,256]{2,1,0:T(8,128)S(1)}, f32[7,8,256]{2,1,0:T(8,128)S(1)}, u32[]{:S(2)}, u32[]{:S(2)}) collective-permute-start(f32[7,8,256]{2,1,0:T(8,128)S(1)} %get-tuple-element.47), channel_id=1, source_target_pairs={{0,2},{2,0},{4,6},{6,4},{8,10},{10,8},{12,14},{14,12},{16,18},{18,... | collective-permute-start | bytes 172040 | tf_op jit(solution)/shard_map/ppermute | solution.py:442
  4.1 6.5 %collective-permute-start.1 = (f32[7,8,256]{2,1,0:T(8,128)S(1)}, f32[7,8,256]{2,1,0:T(8,128)S(1)}, u32[]{:S(2)}, u32[]{:S(2)}) collective-permute-start(f32[7,8,256]{2,1,0:T(8,128)S(1)} %get-tuple-element.48), channel_id=1, source_target_pairs={{0,0},{2,4},{4,2},{6,8},{8,6},{10,12},{12,10},{14,16},{16,14},{18,... | collective-permute-start | bytes 172040 | tf_op jit(solution)/shard_map/ppermute | solution.py:441
  10.6 5.2 %collective-permute-start.2 = (f32[80,128]{1,0:T(8,128)S(1)}, f32[80,128]{1,0:T(8,128)S(1)}, u32[]{:S(2)}, u32[]{:S(2)}) collective-permute-start(f32[80,128]{1,0:T(8,128)S(1)} %shard_map.105), channel_id=1, source_target_pairs={{0,1},{1,0},{2,3},{3,2},{4,5},{5,4},{6,7},{7,6},{8,9},{9,8},{10,11... | collective-permute-start | bytes 122888 | tf_op jit(solution)/shard_map/ppermute | solution.py:451
  12.9 22.6 %collective-permute-start.8 = (f32[4,64,128]{2,1,0:T(8,128)S(1)}, f32[4,64,128]{2,1,0:T(8,128)S(1)}, u32[]{:S(2)}, u32[]{:S(2)}) collective-permute-start(f32[4,64,128]{2,1,0:T(8,128)S(1)} %get-tuple-element.65), channel_id=1, source_target_pairs={{0,16},{2,18},{4,20},{6,22},{8,24},{10,26},{12,28},{14,30},{16,0},... | collective-permute-start | bytes 393224 | tf_op jit(solution)/shard_map/ppermute | solution.py:410
  13.0 23.0 %collective-permute-start.9 = (f32[4,64,128]{2,1,0:T(8,128)S(1)}, f32[4,64,128]{2,1,0:T(8,128)S(1)}, u32[]{:S(2)}, u32[]{:S(2)}) collective-permute-start(f32[4,64,128]{2,1,0:T(8,128)S(1)} %get-tuple-element.66), channel_id=1, source_target_pairs={{0,20},{2,22},{4,16},{6,18},{8,28},{10,30},{12,24},{14,26},{16,4},... | collective-permute-start | bytes 393224 | tf_op jit(solution)/shard_map/ppermute | solution.py:410
  18.5 1.4 %collective-permute-start.4 = (f32[16,8,128]{2,1,0:T(8,128)S(1)}, f32[16,8,128]{2,1,0:T(8,128)S(1)}, u32[]{:S(2)}, u32[]{:S(2)}) collective-permute-start(f32[16,8,128]{2,1,0:T(8,128)S(1)} %get-tuple-element.58.own_ref), channel_id=1, source_target_pairs={{0,2},{2,0},{4,6},{6,4},{8,10},{10,8},{12,14},{14,12},{16,18},{18,... | collective-permute-start | bytes 196616 | tf_op jit(solution)/shard_map/ppermute | solution.py:466
  20.0 4.7 %collective-permute-start.12 = (f32[8,128]{1,0:T(8,128)S(1)}, f32[8,128]{1,0:T(8,128)S(1)}, u32[]{:S(2)}, u32[]{:S(2)}) collective-permute-start(f32[8,128]{1,0:T(8,128)S(1)} %get-tuple-element.70), channel_id=1, source_target_pairs={{0,16},{2,18},{4,20},{6,22},{8,24},{10,26},{12,28},{14,30},{16,0},... | collective-permute-start | bytes 12296 | tf_op jit(solution)/shard_map/ppermute | solution.py:410
  20.4 6.7 %collective-permute-start.13 = (f32[8,128]{1,0:T(8,128)S(1)}, f32[8,128]{1,0:T(8,128)S(1)}, u32[]{:S(2)}, u32[]{:S(2)}) collective-permute-start(f32[8,128]{1,0:T(8,128)S(1)} %get-tuple-element.71), channel_id=1, source_target_pairs={{0,20},{2,22},{4,16},{6,18},{8,28},{10,30},{12,24},{14,26},{16,4},... | collective-permute-start | bytes 12296 | tf_op jit(solution)/shard_map/ppermute | solution.py:410
  23.7 5.1 %collective-permute-start.14 = (f32[8,128]{1,0:T(8,128)S(1)}, f32[8,128]{1,0:T(8,128)S(1)}, u32[]{:S(2)}, u32[]{:S(2)}) collective-permute-start(f32[8,128]{1,0:T(8,128)S(1)} %get-tuple-element.72), channel_id=1, source_target_pairs={{0,24},{2,26},{4,28},{6,30},{8,16},{10,18},{12,20},{14,22},{16,8},... | collective-permute-start | bytes 12296 | tf_op jit(solution)/shard_map/ppermute | solution.py:410
  24.7 6.3 %collective-permute-start.15 = (f32[8,128]{1,0:T(8,128)S(1)}, f32[8,128]{1,0:T(8,128)S(1)}, u32[]{:S(2)}, u32[]{:S(2)}) collective-permute-start(f32[8,128]{1,0:T(8,128)S(1)} %get-tuple-element.73), channel_id=1, source_target_pairs={{0,28},{2,30},{4,24},{6,26},{8,20},{10,22},{12,16},{14,18},{16,12}... | collective-permute-start | bytes 12296 | tf_op jit(solution)/shard_map/ppermute | solution.py:410
  27.1 21.8 %collective-permute-start.5 = (f32[4,72,128]{2,1,0:T(8,128)S(1)}, f32[4,72,128]{2,1,0:T(8,128)S(1)}, u32[]{:S(2)}, u32[]{:S(2)}) collective-permute-start(f32[4,72,128]{2,1,0:T(8,128)S(1)} %get-tuple-element.62), channel_id=1, source_target_pairs={{0,4},{2,6},{4,0},{6,2},{8,12},{10,14},{12,8},{14,10},{16,20},{18,... | collective-permute-start | bytes 442376 | tf_op jit(solution)/shard_map/ppermute | solution.py:410
  28.9 20.0 %collective-permute-start.6 = (f32[4,72,128]{2,1,0:T(8,128)S(1)}, f32[4,72,128]{2,1,0:T(8,128)S(1)}, u32[]{:S(2)}, u32[]{:S(2)}) collective-permute-start(f32[4,72,128]{2,1,0:T(8,128)S(1)} %get-tuple-element.63), channel_id=1, source_target_pairs={{0,8},{2,10},{4,12},{6,14},{8,0},{10,2},{12,4},{14,6},{16,24},{18,... | collective-permute-start | bytes 442376 | tf_op jit(solution)/shard_map/ppermute | solution.py:410
  31.0 17.9 %collective-permute-start.7 = (f32[4,72,128]{2,1,0:T(8,128)S(1)}, f32[4,72,128]{2,1,0:T(8,128)S(1)}, u32[]{:S(2)}, u32[]{:S(2)}) collective-permute-start(f32[4,72,128]{2,1,0:T(8,128)S(1)} %get-tuple-element.64), channel_id=1, source_target_pairs={{0,12},{2,14},{4,8},{6,10},{8,4},{10,6},{12,0},{14,2},{16,28},{18,... | collective-permute-start | bytes 442376 | tf_op jit(solution)/shard_map/ppermute | solution.py:410
  35.4 10.7 %collective-permute-start.10 = (f32[4,64,128]{2,1,0:T(8,128)S(1)}, f32[4,64,128]{2,1,0:T(8,128)S(1)}, u32[]{:S(2)}, u32[]{:S(2)}) collective-permute-start(f32[4,64,128]{2,1,0:T(8,128)S(1)} %get-tuple-element.67), channel_id=1, source_target_pairs={{0,24},{2,26},{4,28},{6,30},{8,16},{10,18},{12,20},{14,22},{16,8},... | collective-permute-start | bytes 393224 | tf_op jit(solution)/shard_map/ppermute | solution.py:410
  35.9 12.9 %collective-permute-start.11 = (f32[4,64,128]{2,1,0:T(8,128)S(1)}, f32[4,64,128]{2,1,0:T(8,128)S(1)}, u32[]{:S(2)}, u32[]{:S(2)}) collective-permute-start(f32[4,64,128]{2,1,0:T(8,128)S(1)} %get-tuple-element.68), channel_id=1, source_target_pairs={{0,28},{2,30},{4,24},{6,26},{8,20},{10,22},{12,16},{14,18},{16,12}... | collective-permute-start | bytes 393224 | tf_op jit(solution)/shard_map/ppermute | solution.py:410
where the time goes:
time: 51.1 us; the launch traced here: 51 us
  starting transfers between devices  26.7 us (52%)
  waiting for transfers between devices  14.8 us (29%)
  Pallas kernels  8.78 us (17%)
  between operations  0.71 us (1%)
    ppermute x11, starting transfers between devices, chip_swap(): return lax.ppermute(value, 'slab', [(i, i ^ 2 * k) for i in range(slabs)])  21 us
    ppermute x11, waiting for transfers between devices, chip_swap(): return lax.ppermute(value, 'slab', [(i, i ^ 2 * k) for i in range(slabs)])  10.8 us
    pallas_call x6, Pallas kernels, call(): pl.pallas_call(kernel, out_shape=out_shape, in_specs=in_specs, out_specs=...  8.78 us
    ppermute x1, starting transfers between devices, shards(): edge_b = lax.ppermute(edge_b, 'slab', swaps(slabs, True))  3.37 us
    ppermute x1, waiting for transfers between devices, shards(): edge_b = lax.ppermute(edge_b, 'slab', swaps(slabs, True))  3.1 us
    ppermute x1, starting transfers between devices, shards(): side_c = lax.ppermute(side, 'col', swaps(cols, False))  1.58 us
  transfers between devices with their start and end apart: 16, of which 5 were waited for; matrix products, arithmetic and copies ran while one was open for 0% of the time, Pallas kernels for 13%

commit v1 on v0

--- a/solution.py
+++ b/solution.py
@@ -212,22 +212,20 @@
         fill(other_ref)
 
 
-def rows_kernel(own_ref, other_ref, *rest):
-    near = [ref for ref in rest if len(ref.shape) == 3]
-    rest = rest[len(near) // 2 :]
-    near, (local, *far) = near[len(near) // 2 :], [ref for ref in rest if len(ref.shape) == 2]
+def rows_kernel(late_k, early_k, own_ref, other_ref, *rest):
+    local_ref, *outs = rest[len(late_k) :]
     me = lax.axis_index("slab")
-    chip, core = me // 2, me % 2
-    for k in range(len(near) + len(far) + 1):
-        at = (chip ^ k) * 2 + core
-        rows = jnp.where(core == 0, own_ref[at], other_ref[at])
-        if k == 0:
-            local[...] = rows
-        elif k <= len(near):
-            ref = near[k - 1]
-            ref[0, ref.shape[1] - rows.shape[0] :] = rows
-        else:
-            far[k - len(near) - 1][...] = rows
+
+    def rows(k):
+        at = ((me // 2) ^ k) * 2 + me % 2
+        return jnp.where(me % 2 == 0, own_ref[at], other_ref[at])
+
+    local_ref[...] = rows(0)
+    for k, ref in zip(late_k, outs):
+        value = rows(k)
+        ref[0, ref.shape[1] - value.shape[0] :] = value
+    for k, ref in zip(early_k, outs[len(late_k) :]):
+        ref[...] = rows(k)
 
 
 def side_kernel(side_ref, a_ref, b_ref, out_ref):
@@ -380,6 +378,13 @@
     return jax.ShapeDtypeStruct(shape, jnp.int32)
 
 
+def shifts(size):
+    return [
+        (i, i + 2 if i + 2 < size else i - 1) if i % 2 else (i, i - 2 if i >= 2 else i + 1)
+        for i in range(size)
+    ]
+
+
 def swaps(size, odd):
     if not odd:
         return [(i, i ^ 1) for i in range(size)]
@@ -388,7 +393,8 @@
 
 def distances(slabs):
     chips = slabs // 2
-    return list(range(1, chips // 2)), list(range(chips // 2, chips))
+    early = range(chips // 2, chips - max(1, chips // 8))
+    return [k for k in range(1, chips) if k not in early], list(early)
 
 
 def shards(
@@ -404,7 +410,7 @@
 
     tall = height + 2 * EDGE
     tail = STEPS * CAP
-    near_k, far_k = distances(slabs)
+    late_k, early_k = distances(slabs)
 
     def chip_swap(value, k):
         return lax.ppermute(value, "slab", [(i, i ^ (2 * k)) for i in range(slabs)])
@@ -438,11 +444,12 @@
             pltpu.SemaphoreType.DMA((4,)),
         ],
     )
-    edge_b = lax.ppermute(edge_b, "slab", swaps(slabs, True))
+    edge_b = lax.ppermute(edge_b, "slab", shifts(slabs))
+    edge_b = lax.ppermute(edge_b, "slab", swaps(slabs, False))
     edge_a = lax.ppermute(edge_a, "slab", swaps(slabs, False))
     packed = call(
         pack_kernel,
-        tuple(f32(CAP, count + (tail if k in near_k else 0), cells) for k in range(chips)),
+        tuple(f32(CAP, count + (tail if k in late_k else 0), cells) for k in range(chips)),
         [SMEM, VMEM, VMEM],
         (VMEM,) * chips,
         (slot, held, hopped),
@@ -450,7 +457,9 @@
     side = call(side_kernel, f32(tall, LANES), [VMEM] * 3, VMEM, (side, edge_a, edge_b))
     side_c = lax.ppermute(side, "col", swaps(cols, False))
     side_d = lax.ppermute(side, "col", swaps(cols, True)) if cols > 2 else side_c
-    far = [chip_swap(packed[k], k) for k in far_k]
+    blocks = {0: packed[0]}
+    for k in early_k:
+        blocks[k] = chip_swap(packed[k], k)
 
     result, rows = call(
         fracture_kernel,
@@ -464,23 +473,25 @@
         [pltpu.VMEM((STEPS, width // LANES, height, LANES), jnp.float32)],
     )
     other_rows = lax.ppermute(rows, "slab", swaps(slabs, False))
-    filled = call(
-        rows_kernel,
-        tuple(f32(CAP, count + tail, cells) for k in near_k) + (f32(tail, cells),) * (1 + len(far_k)),
-        [VMEM] * (2 + len(near_k)),
+    local_rows, *filled = call(
+        functools.partial(rows_kernel, late_k, early_k),
+        (f32(tail, cells),)
+        + (f32(CAP, count + tail, cells),) * len(late_k)
+        + (f32(tail, cells),) * len(early_k),
+        [VMEM] * (2 + len(late_k)),
         (VMEM,) * chips,
-        (rows, other_rows, *(packed[k] for k in near_k)),
-        aliases={2 + i: i for i in range(len(near_k))},
-    )
-    near, (local_rows, *far_rows) = filled[: len(near_k)], filled[len(near_k) :]
-    near = [chip_swap(value, k) for value, k in zip(near, near_k)]
-    far_rows = [chip_swap(value, k) for value, k in zip(far_rows, far_k)]
+        (rows, other_rows, *(packed[k] for k in late_k)),
+        aliases={2 + i: 1 + i for i in range(len(late_k))},
+    )
+    for k, value in zip(late_k, filled):
+        blocks[k] = chip_swap(value, k)
+    loose = [chip_swap(value, k) for k, value in zip(early_k, filled[len(late_k) :])]
     shells_new = call(
         final_kernel,
         f32(new_slots, count, cells),
-        [SMEM] + [VMEM] * (3 + chips + 1 + len(far_k)),
+        [SMEM] + [VMEM] * (3 + chips + 1 + len(early_k)),
         ANY,
-        (recv, cap_row, trans_row, inverse, packed[0], *near, *far, local_rows, *far_rows),
+        (recv, cap_row, trans_row, inverse, *(blocks[k] for k in range(chips)), local_rows, *loose),
         [
             pltpu.VMEM((chips * CAP, count, cells), jnp.float32),
             pltpu.VMEM((chips, tail, cells), jnp.float32),

time: 51.1 us -> 47.1 us (0.922)
  starting transfers between devices: 26.7 us -> 17 us
  waiting for transfers between devices: 14.8 us -> 20.3 us
    ppermute x11 -> x10, starting transfers between devices: 21 us -> 13.9 us  [chip_swap(): return lax.ppermute(value, 'slab', [(i, i ^ 2 * k) for i in range(slabs)])]
    ppermute x11 -> x10, waiting for transfers between devices: 10.8 us -> 13.7 us  [chip_swap(): return lax.ppermute(value, 'slab', [(i, i ^ 2 * k) for i in range(slabs)])]
    ppermute x1, waiting for transfers between devices: 0.01 us -> 2.48 us  [shards(): side_c = lax.ppermute(side, 'col', swaps(cols, False))]
    ppermute x1 -> x2, starting transfers between devices: 3.37 us -> 1.44 us  [the longest x1 1.43 us: shards(): edge_b = lax.ppermute(edge_b, 'slab', shifts(slabs))]
    ppermute x1, starting transfers between devices: 0.55 us -> 0.01 us  [shards(): other_rows = lax.ppermute(rows, 'slab', swaps(slabs, False))]
    ppermute x1 -> x2, waiting for transfers between devices: 3.1 us -> 2.8 us  [the longest x1 2.8 us: shards(): edge_b = lax.ppermute(edge_b, 'slab', shifts(slabs))]
  transfers between devices with their start and end apart: 16 -> 16, of which waited for: 5 -> 6; matrix products, arithmetic and copies ran while one was open for 0% -> 0% of each run, Pallas kernels for 13% -> 14%
where the time goes in v1:
time: 47.1 us; the launch traced here: 46.7 us
  waiting for transfers between devices  20.3 us (43%)
  starting transfers between devices  17 us (36%)
  Pallas kernels  8.79 us (19%)
  between operations  0.7 us (1%)
    ppermute x10, starting transfers between devices, chip_swap(): return lax.ppermute(value, 'slab', [(i, i ^ 2 * k) for i in range(slabs)])  13.9 us
    ppermute x10, waiting for transfers between devices, chip_swap(): return lax.ppermute(value, 'slab', [(i, i ^ 2 * k) for i in range(slabs)])  13.7 us
    pallas_call x6, Pallas kernels, call(): pl.pallas_call(kernel, out_shape=out_shape, in_specs=in_specs, out_specs=...  8.79 us
    ppermute x1, waiting for transfers between devices, shards(): edge_b = lax.ppermute(edge_b, 'slab', shifts(slabs))  2.8 us
    ppermute x1, waiting for transfers between devices, shards(): side_c = lax.ppermute(side, 'col', swaps(cols, False))  2.48 us
    ppermute x1, starting transfers between devices, shards(): side_c = lax.ppermute(side, 'col', swaps(cols, False))  1.58 us
    ppermute x1, starting transfers between devices, shards(): edge_b = lax.ppermute(edge_b, 'slab', shifts(slabs))  1.43 us
    ppermute x1, waiting for transfers between devices, shards(): other_rows = lax.ppermute(rows, 'slab', swaps(slabs, False))  1.25 us
  transfers between devices with their start and end apart: 16, of which 6 were waited for; matrix products, arithmetic and copies ran while one was open for 0% of the time, Pallas kernels for 14%

profile of v1, /device:TPU:16, one launch (start us, length us, event | category | flops | bytes accessed | tf_op | source)
XLA Modules:
  0.0 46.7 jit_solution(12946408448665379646)
XLA Ops:
  0.6 0.1 collective-permute-start.4
  0.7 3.3 %shard_map.104 = (f32[64,128]{1,0:T(8,128)S(1)}, f32[1,128]{1,0:T(1,128)S(1)}, s32[1,64]{1,0:T(1,128)S(1)}, s32[1,64]{1,0:T(1,128)S(1)}, s32[1,32]{1,0:T(1,128)S...) custom-call(f32[1,64]{1,0:T(1,128)} %bitcast.7, ...), custom_call_target="tpu_custom_call" | custom-call | tf_op jit(solution)/shard_map/pallas_call | solution.py:362
  4.0 1.4 %collective-permute-start.1 = (f32[7,8,256]{2,1,0:T(8,128)S(1)}, f32[7,8,256]{2,1,0:T(8,128)S(1)}, u32[]{:S(2)}, u32[]{:S(2)}) collective-permute-start(f32[7,8,256]{2,1,0:T(8,128)S(1)} %get-tuple-element.48), channel_id=1, source_target_pairs={{0,2},{2,6},{4,0},{6,10},{8,4},{10,14},{12,8},{14,18},{16,12},{18,... | collective-permute-start | bytes 172040 | tf_op jit(solution)/shard_map/ppermute | solution.py:447
  5.4 0.0 collective-permute-start
  5.4 2.8 %collective-permute-done.1 = f32[7,8,256]{2,1,0:T(8,128)S(1)} collective-permute-done((f32[7,8,256]{2,1,0:T(8,128)S(1)}, f32[7,8,256]{2,1,0:T(8,128)S(1)}, u32[]{:S(2)}, u32[]{:S(2)}) %collective-permute-start.1) | collective-permute-done | bytes 57376 | tf_op jit(solution)/shard_map/ppermute | solution.py:447
  8.2 0.0 collective-permute-start.2
  8.2 0.0 collective-permute-done.4.other_ref
  8.2 0.6 %shard_map.107 = (f32[4,64,128]{2,1,0:T(8,128)S(1)}, f32[4,72,128]{2,1,0:T(8,128)S(1)}, f32[4,72,128]{2,1,0:T(8,128)S(1)}, f32[4,72,128]{2,1,0:T(8,128)S(1)}, f3...) custom-call(s32[1,64]{1,0:T(1,128)S(1)} %get-tuple-element.55.slot_r, ...), custom_call_target="tpu_custom_call" | custom-call | tf_op jit(solution)/shard_map/pallas_call | solution.py:362
  8.9 0.1 collective-permute-start.9
  8.9 4.7 %collective-permute-start.10 = (f32[4,64,128]{2,1,0:T(8,128)S(1)}, f32[4,64,128]{2,1,0:T(8,128)S(1)}, u32[]{:S(2)}, u32[]{:S(2)}) collective-permute-start(f32[4,64,128]{2,1,0:T(8,128)S(1)} %get-tuple-element.67), channel_id=1, source_target_pairs={{0,20},{2,22},{4,16},{6,18},{8,28},{10,30},{12,24},{14,26},{16,4},... | collective-permute-start | bytes 393224 | tf_op jit(solution)/shard_map/ppermute | solution.py:416
  13.7 0.0 collective-permute-done.a_ref
  13.7 0.0 collective-permute-done.2.b_ref
  13.7 0.1 shard_map.105
  13.8 1.6 %collective-permute-start.3 = (f32[80,128]{1,0:T(8,128)S(1)}, f32[80,128]{1,0:T(8,128)S(1)}, u32[]{:S(2)}, u32[]{:S(2)}) collective-permute-start(f32[80,128]{1,0:T(8,128)S(1)} %shard_map.105), channel_id=1, source_target_pairs={{0,1},{1,0},{2,3},{3,2},{4,5},{5,4},{6,7},{7,6},{8,9},{9,8},{10,11... | collective-permute-start | bytes 122888 | tf_op jit(solution)/shard_map/ppermute | solution.py:458
  15.4 2.5 %collective-permute-done.3.c_ref.d_ref = f32[80,128]{1,0:T(8,128)S(1)} collective-permute-done((f32[80,128]{1,0:T(8,128)S(1)}, f32[80,128]{1,0:T(8,128)S(1)}, u32[]{:S(2)}, u32[]{:S(2)}) %collective-permute-start.3) | collective-permute-done | bytes 40992 | tf_op jit(solution)/shard_map/ppermute | solution.py:458
  17.8 2.7 %shard_map.106 = (f32[64,256]{1,0:T(8,128)}, f32[16,8,128]{2,1,0:T(8,128)S(1)}) custom-call(s32[1,64]{1,0:T(1,128)S(1)} %get-tuple-element.38.place_ref, f32[1,128]{1,0:T(1,128)S(1)} %get-tuple-element.39.const_ref, f32[64,256]{1,0:T(8,128)S(1)} %get-tuple-element.40.p_ref, f32[64,256]{1,0:T(8,128)S(1)} %get-tuple-element.41.storage_ref, ...), custom_call_target="tpu_custom_call" | custom-call | tf_op jit(solution)/shard_map/pallas_call | solution.py:362
  20.6 0.0 collective-permute-start.5
  20.6 1.3 %collective-permute-done.5.other_ref = f32[16,8,128]{2,1,0:T(8,128)S(1)} collective-permute-done((f32[16,8,128]{2,1,0:T(8,128)S(1)}, f32[16,8,128]{2,1,0:T(8,128)S(1)}, u32[]{:S(2)}, u32[]{:S(2)}) %collective-permute-start.5) | collective-permute-done | bytes 65568 | tf_op jit(solution)/shard_map/ppermute | solution.py:475
  21.8 0.4 collective-permute-start.13
  22.2 1.7 %collective-permute-start.14 = (f32[8,128]{1,0:T(8,128)S(1)}, f32[8,128]{1,0:T(8,128)S(1)}, u32[]{:S(2)}, u32[]{:S(2)}) collective-permute-start(f32[8,128]{1,0:T(8,128)S(1)} %get-tuple-element.72), channel_id=1, source_target_pairs={{0,20},{2,22},{4,16},{6,18},{8,28},{10,30},{12,24},{14,26},{16,4},... | collective-permute-start | bytes 12296 | tf_op jit(solution)/shard_map/ppermute | solution.py:416
  23.9 0.5 collective-permute-start.15
  24.3 2.1 %collective-permute-done.13.rest_9_ = f32[8,128]{1,0:T(8,128)S(1)} collective-permute-done((f32[8,128]{1,0:T(8,128)S(1)}, f32[8,128]{1,0:T(8,128)S(1)}, u32[]{:S(2)}, u32[]{:S(2)}) %collective-permute-start.13) | collective-permute-done | bytes 4128 | tf_op jit(solution)/shard_map/ppermute | solution.py:416
  26.4 0.3 collective-permute-start.6
  26.7 0.9 %collective-permute-done.14.rest_10_ = f32[8,128]{1,0:T(8,128)S(1)} collective-permute-done((f32[8,128]{1,0:T(8,128)S(1)}, f32[8,128]{1,0:T(8,128)S(1)}, u32[]{:S(2)}, u32[]{:S(2)}) %collective-permute-start.14) | collective-permute-done | bytes 4128 | tf_op jit(solution)/shard_map/ppermute | solution.py:416
  27.7 1.6 %collective-permute-start.7 = (f32[4,72,128]{2,1,0:T(8,128)S(1)}, f32[4,72,128]{2,1,0:T(8,128)S(1)}, u32[]{:S(2)}, u32[]{:S(2)}) collective-permute-start(f32[4,72,128]{2,1,0:T(8,128)S(1)} %get-tuple-element.64), channel_id=1, source_target_pairs={{0,8},{2,10},{4,12},{6,14},{8,0},{10,2},{12,4},{14,6},{16,24},{18,... | collective-permute-start | bytes 442376 | tf_op jit(solution)/shard_map/ppermute | solution.py:416
  29.3 0.0 collective-permute-done.15.rest_11_
  29.3 1.0 %collective-permute-start.8 = (f32[4,72,128]{2,1,0:T(8,128)S(1)}, f32[4,72,128]{2,1,0:T(8,128)S(1)}, u32[]{:S(2)}, u32[]{:S(2)}) collective-permute-start(f32[4,72,128]{2,1,0:T(8,128)S(1)} %get-tuple-element.65), channel_id=1, source_target_pairs={{0,12},{2,14},{4,8},{6,10},{8,4},{10,6},{12,0},{14,2},{16,28},{18,... | collective-permute-start | bytes 442376 | tf_op jit(solution)/shard_map/ppermute | solution.py:416
  30.3 0.0 collective-permute-done.9.rest_4_
  30.3 1.5 %collective-permute-start.12 = (f32[4,72,128]{2,1,0:T(8,128)S(1)}, f32[4,72,128]{2,1,0:T(8,128)S(1)}, u32[]{:S(2)}, u32[]{:S(2)}) collective-permute-start(f32[4,72,128]{2,1,0:T(8,128)S(1)} %get-tuple-element.69), channel_id=1, source_target_pairs={{0,28},{2,30},{4,24},{6,26},{8,20},{10,22},{12,16},{14,18},{16,12}... | collective-permute-start | bytes 442376 | tf_op jit(solution)/shard_map/ppermute | solution.py:416
  31.8 0.0 collective-permute-done.10.rest_5_
  31.8 2.1 %collective-permute-start.11 = (f32[4,64,128]{2,1,0:T(8,128)S(1)}, f32[4,64,128]{2,1,0:T(8,128)S(1)}, u32[]{:S(2)}, u32[]{:S(2)}) collective-permute-start(f32[4,64,128]{2,1,0:T(8,128)S(1)} %get-tuple-element.68), channel_id=1, source_target_pairs={{0,24},{2,26},{4,28},{6,30},{8,16},{10,18},{12,20},{14,22},{16,8},... | collective-permute-start | bytes 393224 | tf_op jit(solution)/shard_map/ppermute | solution.py:416
  33.9 10.7 %collective-permute-done.11.rest_6_ = f32[4,64,128]{2,1,0:T(8,128)S(1)} collective-permute-done((f32[4,64,128]{2,1,0:T(8,128)S(1)}, f32[4,64,128]{2,1,0:T(8,128)S(1)}, u32[]{:S(2)}, u32[]{:S(2)}) %collective-permute-start.11) | collective-permute-done | bytes 131104 | tf_op jit(solution)/shard_map/ppermute | solution.py:416
  44.6 0.0 collective-permute-done.6.rest_1_
  44.6 0.0 collective-permute-done.7.rest_2_
  44.6 0.0 collective-permute-done.8.rest_3_
  44.6 0.0 collective-permute-done.12.rest_7_
  44.7 2.1 %shard_map.109 = f32[32,64,128]{2,1,0:T(8,128)} custom-call(s32[1,32]{1,0:T(1,128)S(1)} %get-tuple-element.51.recv_ref, f32[1,64]{1,0:T(1,128)S(1)} %get-tuple-element.52.cap_ref, f32[1,64]{1,0:T(1,128)S(1)} %get-tuple-element.53.trans_ref, f32[64,128]{1,0:T(8,128)S(1)} %get-tuple-element.54.inv_ref, f32[4,64,128]{2,1,0:T(8,128)S(1)} %get-tuple-element.57.rest_0_, ...), custom_call_target="tpu_custom_call" | custom-call | tf_op jit(solution)/shard_map/pallas_call | solution.py:362
  (1 shorter events, 0.0 us)
Async XLA Ops:
  0.6 7.6 %collective-permute-start.4 = (f32[64,64,128]{2,1,0:T(8,128)}, f32[64,64,128]{2,1,0:T(8,128)S(1)}, u32[]{:S(2)}, u32[]{:S(2)}) collective-permute-start(f32[64,64,128]{2,1,0:T(8,128)} %bitcast.4), channel_id=1, source_target_pairs={{0,2},{2,0},{4,6},{6,4},{8,10},{10,8},{12,14},{14,12},{16,18},{18,... | collective-permute-start | bytes 6291464 | tf_op jit(solution)/shard_map/ppermute | solution.py:418
  4.0 4.2 %collective-permute-start.1 = (f32[7,8,256]{2,1,0:T(8,128)S(1)}, f32[7,8,256]{2,1,0:T(8,128)S(1)}, u32[]{:S(2)}, u32[]{:S(2)}) collective-permute-start(f32[7,8,256]{2,1,0:T(8,128)S(1)} %get-tuple-element.48), channel_id=1, source_target_pairs={{0,2},{2,6},{4,0},{6,10},{8,4},{10,14},{12,8},{14,18},{16,12},{18,... | collective-permute-start | bytes 172040 | tf_op jit(solution)/shard_map/ppermute | solution.py:447
  5.4 8.3 %collective-permute-start = (f32[7,8,256]{2,1,0:T(8,128)S(1)}, f32[7,8,256]{2,1,0:T(8,128)S(1)}, u32[]{:S(2)}, u32[]{:S(2)}) collective-permute-start(f32[7,8,256]{2,1,0:T(8,128)S(1)} %get-tuple-element.47), channel_id=1, source_target_pairs={{0,2},{2,0},{4,6},{6,4},{8,10},{10,8},{12,14},{14,12},{16,18},{18,... | collective-permute-start | bytes 172040 | tf_op jit(solution)/shard_map/ppermute | solution.py:449
  8.2 5.5 %collective-permute-start.2 = (f32[7,8,256]{2,1,0:T(8,128)S(1)}, f32[7,8,256]{2,1,0:T(8,128)S(1)}, u32[]{:S(2)}, u32[]{:S(2)}) collective-permute-start(f32[7,8,256]{2,1,0:T(8,128)S(1)} %collective-permute-done.1), channel_id=1, source_target_pairs={{0,2},{2,0},{4,6},{6,4},{8,10},{10,8},{12,14},{14,12},{16,18},{18,... | collective-permute-start | bytes 172040 | tf_op jit(solution)/shard_map/ppermute | solution.py:448
  8.9 21.4 %collective-permute-start.9 = (f32[4,64,128]{2,1,0:T(8,128)S(1)}, f32[4,64,128]{2,1,0:T(8,128)S(1)}, u32[]{:S(2)}, u32[]{:S(2)}) collective-permute-start(f32[4,64,128]{2,1,0:T(8,128)S(1)} %get-tuple-element.66), channel_id=1, source_target_pairs={{0,16},{2,18},{4,20},{6,22},{8,24},{10,26},{12,28},{14,30},{16,0},... | collective-permute-start | bytes 393224 | tf_op jit(solution)/shard_map/ppermute | solution.py:416
  8.9 22.9 %collective-permute-start.10 = (f32[4,64,128]{2,1,0:T(8,128)S(1)}, f32[4,64,128]{2,1,0:T(8,128)S(1)}, u32[]{:S(2)}, u32[]{:S(2)}) collective-permute-start(f32[4,64,128]{2,1,0:T(8,128)S(1)} %get-tuple-element.67), channel_id=1, source_target_pairs={{0,20},{2,22},{4,16},{6,18},{8,28},{10,30},{12,24},{14,26},{16,4},... | collective-permute-start | bytes 393224 | tf_op jit(solution)/shard_map/ppermute | solution.py:416
  13.8 4.1 %collective-permute-start.3 = (f32[80,128]{1,0:T(8,128)S(1)}, f32[80,128]{1,0:T(8,128)S(1)}, u32[]{:S(2)}, u32[]{:S(2)}) collective-permute-start(f32[80,128]{1,0:T(8,128)S(1)} %shard_map.105), channel_id=1, source_target_pairs={{0,1},{1,0},{2,3},{3,2},{4,5},{5,4},{6,7},{7,6},{8,9},{9,8},{10,11... | collective-permute-start | bytes 122888 | tf_op jit(solution)/shard_map/ppermute | solution.py:458
  20.6 1.3 %collective-permute-start.5 = (f32[16,8,128]{2,1,0:T(8,128)S(1)}, f32[16,8,128]{2,1,0:T(8,128)S(1)}, u32[]{:S(2)}, u32[]{:S(2)}) collective-permute-start(f32[16,8,128]{2,1,0:T(8,128)S(1)} %get-tuple-element.58.own_ref), channel_id=1, source_target_pairs={{0,2},{2,0},{4,6},{6,4},{8,10},{10,8},{12,14},{14,12},{16,18},{18,... | collective-permute-start | bytes 196616 | tf_op jit(solution)/shard_map/ppermute | solution.py:475
  21.8 4.6 %collective-permute-start.13 = (f32[8,128]{1,0:T(8,128)S(1)}, f32[8,128]{1,0:T(8,128)S(1)}, u32[]{:S(2)}, u32[]{:S(2)}) collective-permute-start(f32[8,128]{1,0:T(8,128)S(1)} %get-tuple-element.71), channel_id=1, source_target_pairs={{0,16},{2,18},{4,20},{6,22},{8,24},{10,26},{12,28},{14,30},{16,0},... | collective-permute-start | bytes 12296 | tf_op jit(solution)/shard_map/ppermute | solution.py:416
  22.2 5.4 %collective-permute-start.14 = (f32[8,128]{1,0:T(8,128)S(1)}, f32[8,128]{1,0:T(8,128)S(1)}, u32[]{:S(2)}, u32[]{:S(2)}) collective-permute-start(f32[8,128]{1,0:T(8,128)S(1)} %get-tuple-element.72), channel_id=1, source_target_pairs={{0,20},{2,22},{4,16},{6,18},{8,28},{10,30},{12,24},{14,26},{16,4},... | collective-permute-start | bytes 12296 | tf_op jit(solution)/shard_map/ppermute | solution.py:416
  23.9 5.4 %collective-permute-start.15 = (f32[8,128]{1,0:T(8,128)S(1)}, f32[8,128]{1,0:T(8,128)S(1)}, u32[]{:S(2)}, u32[]{:S(2)}) collective-permute-start(f32[8,128]{1,0:T(8,128)S(1)} %get-tuple-element.73), channel_id=1, source_target_pairs={{0,24},{2,26},{4,28},{6,30},{8,16},{10,18},{12,20},{14,22},{16,8},... | collective-permute-start | bytes 12296 | tf_op jit(solution)/shard_map/ppermute | solution.py:416
  26.4 18.2 %collective-permute-start.6 = (f32[4,72,128]{2,1,0:T(8,128)S(1)}, f32[4,72,128]{2,1,0:T(8,128)S(1)}, u32[]{:S(2)}, u32[]{:S(2)}) collective-permute-start(f32[4,72,128]{2,1,0:T(8,128)S(1)} %get-tuple-element.63), channel_id=1, source_target_pairs={{0,4},{2,6},{4,0},{6,2},{8,12},{10,14},{12,8},{14,10},{16,20},{18,... | collective-permute-start | bytes 442376 | tf_op jit(solution)/shard_map/ppermute | solution.py:416
  27.7 17.0 %collective-permute-start.7 = (f32[4,72,128]{2,1,0:T(8,128)S(1)}, f32[4,72,128]{2,1,0:T(8,128)S(1)}, u32[]{:S(2)}, u32[]{:S(2)}) collective-permute-start(f32[4,72,128]{2,1,0:T(8,128)S(1)} %get-tuple-element.64), channel_id=1, source_target_pairs={{0,8},{2,10},{4,12},{6,14},{8,0},{10,2},{12,4},{14,6},{16,24},{18,... | collective-permute-start | bytes 442376 | tf_op jit(solution)/shard_map/ppermute | solution.py:416
  29.3 15.3 %collective-permute-start.8 = (f32[4,72,128]{2,1,0:T(8,128)S(1)}, f32[4,72,128]{2,1,0:T(8,128)S(1)}, u32[]{:S(2)}, u32[]{:S(2)}) collective-permute-start(f32[4,72,128]{2,1,0:T(8,128)S(1)} %get-tuple-element.65), channel_id=1, source_target_pairs={{0,12},{2,14},{4,8},{6,10},{8,4},{10,6},{12,0},{14,2},{16,28},{18,... | collective-permute-start | bytes 442376 | tf_op jit(solution)/shard_map/ppermute | solution.py:416
  30.3 14.4 %collective-permute-start.12 = (f32[4,72,128]{2,1,0:T(8,128)S(1)}, f32[4,72,128]{2,1,0:T(8,128)S(1)}, u32[]{:S(2)}, u32[]{:S(2)}) collective-permute-start(f32[4,72,128]{2,1,0:T(8,128)S(1)} %get-tuple-element.69), channel_id=1, source_target_pairs={{0,28},{2,30},{4,24},{6,26},{8,20},{10,22},{12,16},{14,18},{16,12}... | collective-permute-start | bytes 442376 | tf_op jit(solution)/shard_map/ppermute | solution.py:416
  31.8 12.8 %collective-permute-start.11 = (f32[4,64,128]{2,1,0:T(8,128)S(1)}, f32[4,64,128]{2,1,0:T(8,128)S(1)}, u32[]{:S(2)}, u32[]{:S(2)}) collective-permute-start(f32[4,64,128]{2,1,0:T(8,128)S(1)} %get-tuple-element.68), channel_id=1, source_target_pairs={{0,24},{2,26},{4,28},{6,30},{8,16},{10,18},{12,20},{14,22},{16,8},... | collective-permute-start | bytes 393224 | tf_op jit(solution)/shard_map/ppermute | solution.py:416

commit v2 on v1

--- a/solution.py
+++ b/solution.py
@@ -72,7 +72,22 @@
         rhs = rhs + alpha * down(rhs) + gamma * up(rhs)
         low, high = alpha * down(low), gamma * up(high)
         step *= 2
-    return rhs / diag, cap, trans
+    return rhs / diag, cap
+
+
+def sent_blocks(table, old_slots, slabs):
+    me = lax.axis_index("slab")
+    total = table.shape[1]
+    new_slots = total // slabs
+    anchor, local = split_by(table, old_slots)
+    dest, within = split_by(iota((1, total), 1), new_slots)
+    mine = anchor == me - me % 2
+    seen = jnp.where(mine, 1, 0)
+    shift = 1
+    while shift < new_slots:
+        seen = seen + jnp.where(within >= shift, pltpu.roll(seen, shift, axis=1), 0)
+        shift *= 2
+    return jnp.where(mine, dest * CAP + jnp.minimum(seen, CAP) - 1, -1), local
 
 
 def pack_sides(get, rows):
@@ -91,9 +106,9 @@
 
 def base_kernel(
     cap_hbm, trans_hbm, table_hbm, block_hbm, shells_hbm, p_hbm, storage_hbm, t_hbm, source_hbm,
-    inv_ref, const_ref, slot_ref, place_ref, recv_ref, cap_ref, trans_ref, held,
-    p_ref, storage_ref, t_ref, source_ref, b1_ref, b2_ref, e_ref, a_ref, b_ref, side_ref,
-    tiles, table_ref, block_row, block_ref, sem, chunk_sem,
+    inv_ref, const_ref, slot_ref, table_ref, block_row, cap_ref, trans_ref, held,
+    p_ref, storage_ref, t_ref, source_ref, b1_ref, b2_ref, e_ref, a_ref, b_ref,
+    tiles, block_ref, sem, chunk_sem,
 ):
     me = lax.axis_index("slab")
     slabs = lax.axis_size("slab")
@@ -124,7 +139,7 @@
     for load in loads:
         load.wait()
     cap_row, trans_row = cap_ref[...], trans_ref[...]
-    inverse, cap, _ = inverse_of(cap_row, trans_row)
+    inverse, cap = inverse_of(cap_row, trans_row)
     inv_ref[...] = inverse
     t0 = trans_row[:, 0:1]
     first_row = inverse[0:1, :count] * cap_row
@@ -147,18 +162,13 @@
         for i in range(chunks):
             chunk(i).wait()
 
-            def body(j, carry):
-                for u in range(4):
-                    slot = i * per + j * 4 + u
-                    data = held[slot]
-                    row, half = split_by(block_ref[0, slot], per_row)
-                    at = pl.ds(row, 1)
-                    tiles[0, half, at] = jnp.sum(v1 * data, axis=0, keepdims=True)
-                    tiles[1, half, at] = jnp.sum(v2 * data, axis=0, keepdims=True)
-                    tiles[2, half, at] = on
-                return carry
-
-            lax.fori_loop(0, per // 4, body, 0)
+            for slot in range(i * per, (i + 1) * per):
+                data = held[slot]
+                row, half = split_by(block_ref[0, slot], per_row)
+                at = pl.ds(row, 1)
+                tiles[0, half, at] = jnp.sum(v1 * data, axis=0, keepdims=True)
+                tiles[1, half, at] = jnp.sum(v2 * data, axis=0, keepdims=True)
+                tiles[2, half, at] = on
 
     for i, ref in enumerate((b1_ref, b2_ref, e_ref)):
         ref[...] = jnp.concatenate([tiles[i, h] for h in range(tiles.shape[1])], axis=1)
@@ -168,29 +178,8 @@
         top, bottom = ref[0:EDGE, :], ref[height - EDGE : height, :]
         a_ref[f] = jnp.where(even, bottom, top)
         b_ref[f] = jnp.where(even, top, bottom)
-    side_ref[...] = pack_sides(lambda f: fields[f][...], height)
-
-    table = table_ref[...]
-    total = table.shape[1]
-    new_slots = total // slabs
-    anchor, local = split_by(table, old_slots)
-    lane = iota((1, total), 1)
-    dest, within = split_by(lane, new_slots)
-    rank = jnp.zeros((1, total), jnp.int32)
-    for shift in range(1, new_slots):
-        same = (pltpu.roll(anchor, shift, axis=1) == anchor) & (within >= shift)
-        rank = rank + jnp.where(same, 1, 0)
-    rank = jnp.minimum(rank, CAP - 1)
-    mine = anchor == me - me % 2
-    target = jnp.where(mine, dest * CAP + rank, -1)
+    target, local = sent_blocks(table_ref[...], old_slots, slabs)
     slot_ref[...] = placed(target, local, slabs * CAP)
-    eye = iota((old_slots, old_slots), 0) == iota((old_slots, old_slots), 1)
-    column = column_of(block_row[...].astype(jnp.float32), eye)
-    owner = iota((old_slots, total), 0) == local
-    here = jnp.sum(jnp.where(owner, column, 0.0), axis=0, keepdims=True)
-    place_ref[...] = placed(target, here, slabs * CAP)
-    recv = ((anchor >> 1) ^ (me // 2)) * CAP + rank
-    recv_ref[...] = placed(lane - me * new_slots, recv, new_slots)
 
 
 def pack_kernel(slot_ref, own_ref, other_ref, *out_refs):
@@ -228,20 +217,43 @@
         ref[...] = rows(k)
 
 
-def side_kernel(side_ref, a_ref, b_ref, out_ref):
-    even = lax.axis_index("slab") % 2 == 0
-    height = side_ref.shape[0]
+def side_kernel(table_ref, block_ref, *rest):
+    *fields, a_ref, b_ref, out_ref, place_ref, recv_ref = rest
+    me, slabs = lax.axis_index("slab"), lax.axis_size("slab")
+    even = me % 2 == 0
+    height = fields[0].shape[0]
     from_a = pack_sides(lambda f: a_ref[f], EDGE)
     from_b = pack_sides(lambda f: b_ref[f], EDGE)
     out_ref[0:EDGE] = jnp.where(even, from_b, from_a)
-    out_ref[EDGE : EDGE + height] = side_ref[...]
+    out_ref[EDGE : EDGE + height] = pack_sides(lambda f: fields[f][...], height)
     out_ref[EDGE + height :] = jnp.where(even, from_a, from_b)
+
+    old_slots = block_ref.shape[1]
+    table = table_ref[...]
+    total = table.shape[1]
+    target, local = sent_blocks(table, old_slots, slabs)
+    eye = iota((old_slots, old_slots), 0) == iota((old_slots, old_slots), 1)
+    column = column_of(block_ref[...].astype(jnp.float32), eye)
+    owner = iota((old_slots, total), 0) == local
+    here = jnp.sum(jnp.where(owner, column, 0.0), axis=0, keepdims=True)
+    place_ref[...] = placed(target, here, slabs * CAP)
+
+    count = recv_ref.shape[1]
+    anchor, _ = split_by(placed(iota((1, total), 1) - me * count, table, count), old_slots)
+    row, above = iota((count, count), 0), iota((count, count), 1)
+    column = column_of(anchor.astype(jnp.float32), row == above)
+    same = (column == anchor.astype(jnp.float32)) & (above < row)
+    rank = row_of(jnp.sum(jnp.where(same, 1.0, 0.0), axis=1, keepdims=True), count)
+    rank = jnp.minimum(rank.astype(jnp.int32), CAP - 1)
+    recv_ref[...] = ((anchor >> 1) ^ (me // 2)) * CAP + rank
 
 
 def fracture_kernel(
     place_ref, const_ref, p_ref, storage_ref, t_ref, source_ref, b1_ref, b2_ref, e_ref,
-    a_ref, b_ref, c_ref, d_ref, out_ref, rows_ref, keep,
+    a_ref, b_ref, c_ref, d_ref, out_ref, rows_ref, keep, place, sem,
 ):
+    table = pltpu.make_async_copy(place_ref, place, sem)
+    table.start()
     me, slabs = lax.axis_index("slab"), lax.axis_size("slab")
     col, cols = lax.axis_index("col"), lax.axis_size("col")
     even, col_even = me % 2 == 0, col % 2 == 0
@@ -293,68 +305,101 @@
                 for h in range(width // LANES):
                     keep[step, h] = mid[:, h * LANES : (h + 1) * LANES]
                 last = p
-            near = next_lane(p)
-            flow_h = half_h * (near + p) * (near - p)
-            near = next_row(p)
-            flow_v = half_v * (near + p) * (near - p)
+            square = p * p
+            if step == STEPS - 1 and sweep == ITERS - 1:
+                break
+            flow_h = half_h * (next_lane(square) - square)
+            flow_v = half_v * (next_row(square) - square)
             flux = flow_h - prev_lane(flow_h) + flow_v - prev_row(flow_v)
             misfit = storage * (p - prev) - flux + coef * p - rhs
             p = p - misfit / (fixed + p * conduct)
-        rhs = source + base2 + ratio * coef * last
-    out_ref[...] = p[EDGE : EDGE + height, :width]
-
-    def body(d, carry):
-        for r in range(CAP):
-            at_row, half = split_by(place_ref[0, d * CAP + r], width // LANES)
-            for step in range(STEPS):
-                rows_ref[d, pl.ds(step * CAP + r, 1)] = keep[step, half, pl.ds(at_row, 1)]
-        return carry
-
-    lax.fori_loop(0, slabs, body, 0)
-
-
-def final_kernel(recv_ref, cap_ref, trans_ref, inv_ref, *rest):
-    *in_refs, out_ref, held, rows, done, sem = rest
-    slots, count = out_ref.shape[:2]
-    blocks = [ref for ref in in_refs if len(ref.shape) == 3]
-    loose = [ref for ref in in_refs if len(ref.shape) == 2]
-    for k, ref in enumerate(blocks):
-        held[pl.ds(k * CAP, CAP)] = ref[:, :count]
-        inside = ref.shape[1] > count
-        rows[k] = ref[0, count:] if inside else loose.pop(0)[...]
-    cap_row = cap_ref[...]
+        if step < STEPS - 1:
+            rhs = source + base2 + ratio * coef * last
+
+    def own(value):
+        return value[EDGE : EDGE + height, :width]
+
+    strip, slab = square[EDGE : EDGE + height], square[:, :width]
+    flow_h = half_h[EDGE : EDGE + height] * (next_lane(strip) - strip)
+    flow_v = half_v[:, :width] * (next_row(slab) - slab)
+    flux = (flow_h - prev_lane(flow_h))[:, :width] + (flow_v - prev_row(flow_v))[EDGE : EDGE + height]
+    p, prev = own(p), own(prev)
+    misfit = own(storage) * (p - prev) - flux + own(coef) * p - own(rhs)
+    out_ref[...] = p - misfit / (own(fixed) + p * own(conduct))
+
+    table.wait()
+    for q in range(rows_ref.shape[0] * CAP):
+        d, r = q // CAP, q % CAP
+        at_row, half = split_by(place[0, q], width // LANES)
+        for step in range(STEPS):
+            rows_ref[d, pl.ds(step * CAP + r, 1)] = keep[step, half, pl.ds(at_row, 1)]
+
+
+def multiply(left, blocks):
+    results = []
+    for first in range(0, len(blocks), 2):
+        parts = []
+        for data in blocks[first : first + 2]:
+            hi = data.astype(jnp.bfloat16)
+            lo = (data - hi.astype(jnp.float32)).astype(jnp.bfloat16)
+            parts.append(jnp.concatenate([hi, lo, hi], axis=0))
+        product = jnp.dot(left, jnp.concatenate(parts, axis=1), preferred_element_type=jnp.float32)
+        results += [product[:, :LANES], product[:, LANES:]]
+    return results
+
+
+def product_kernel(cap_ref, trans_ref, inv_ref, *rest):
+    *blocks, left_ref, m_ref, out_ref = rest
+    count = cap_ref.shape[1]
     inverse = inv_ref[:, :count]
     t0 = trans_ref[:, 0:1]
-    a = inverse * cap_row
+    a = inverse * cap_ref[...]
     couple = inv_ref[:, 0:1] * t0
     couple2 = jnp.sum(a * (inverse[0:1, :] * t0), axis=1, keepdims=True)
     square = jnp.dot(a, a, preferred_element_type=jnp.float32, precision=lax.Precision.HIGHEST)
     high = square.astype(jnp.bfloat16)
     low = (square - high.astype(jnp.float32)).astype(jnp.bfloat16)
     left = jnp.concatenate([high, high, low], axis=1)
-    m1 = jnp.broadcast_to(couple2, (count, LANES))
-    m2 = jnp.broadcast_to(couple, (count, LANES))
-    pair = 2
+    left_ref[...] = left
+    m_ref[0] = jnp.broadcast_to(couple2, (count, LANES))
+    m_ref[1] = jnp.broadcast_to(couple, (count, LANES))
+    for i, ref in enumerate(blocks):
+        for r, value in enumerate(multiply(left, [ref[r, :count] for r in range(CAP)])):
+            out_ref[i * CAP + r] = value
+
+
+def final_kernel(ready_k, tailed_k, loose_k, recv_ref, left_ref, m_ref, product_ref, *rest):
+    *in_refs, out_ref, held, rows, done, recv, recv_sem, sem = rest
+    slots, count = out_ref.shape[:2]
+    table = pltpu.make_async_copy(recv_ref, recv, recv_sem)
+    table.start()
+    for i, k in enumerate(ready_k):
+        held[pl.ds(k * CAP, CAP)] = product_ref[pl.ds(i * CAP, CAP)]
+    left = left_ref[...]
+    for k, ref in zip(tailed_k, in_refs):
+        rows[k] = ref[0, count:]
+        if k not in ready_k:
+            for r, value in enumerate(multiply(left, [ref[r, :count] for r in range(CAP)])):
+                held[k * CAP + r] = value
+    for k, ref in zip(loose_k, in_refs[len(tailed_k) :]):
+        rows[k] = ref[...]
+    m1, m2 = m_ref[0], m_ref[1]
+    group = 4
+    table.wait()
 
     def write(j):
-        part = pl.ds(j * pair, pair)
+        part = pl.ds(j * group, group)
         return pltpu.make_async_copy(done.at[part], out_ref.at[part], sem.at[j])
 
-    for j in range(slots // pair):
-        parts = []
-        for u in range(pair):
-            data = held[recv_ref[0, j * pair + u]]
-            hi = data.astype(jnp.bfloat16)
-            lo = (data - hi.astype(jnp.float32)).astype(jnp.bfloat16)
-            parts.append(jnp.concatenate([hi, lo, hi], axis=0))
-        product = jnp.dot(left, jnp.concatenate(parts, axis=1), preferred_element_type=jnp.float32)
-        for u in range(pair):
-            k, r = split_by(recv_ref[0, j * pair + u], CAP)
+    for j in range(slots // group):
+        for n in range(j * group, (j + 1) * group):
+            index = recv[0, n]
+            k, r = split_by(index, CAP)
             p1 = rows[k, pl.ds(r, 1)]
             p2 = rows[k, pl.ds(r + CAP, 1)]
-            done[j * pair + u] = product[:, u * LANES : (u + 1) * LANES] + m1 * p1 + m2 * p2
+            done[n] = held[index] + m1 * p1 + m2 * p2
         write(j).start()
-    for j in range(slots // pair):
+    for j in range(slots // group):
         write(j).wait()
 
 
@@ -418,17 +463,17 @@
     hopped = lax.ppermute(shells, "slab", swaps(slabs, False))
     plane, edge = f32(height, width), f32(FIELDS, EDGE, width)
     (
-        inverse, const, slot, place, recv, cap_row, trans_row, held,
-        pressure, storage, trans, source, base1, base2, coef, edge_a, edge_b, side,
+        inverse, const, slot, table, block_row, cap_row, trans_row, held,
+        pressure, storage, trans, source, base1, base2, coef, edge_a, edge_b,
     ) = call(
         base_kernel,
         (
-            f32(count, LANES), f32(1, LANES), i32(1, slabs * CAP), i32(1, slabs * CAP),
-            i32(1, new_slots), f32(1, count), f32(1, count), f32(old_slots, count, cells),
-            *(plane,) * 7, edge, edge, f32(height, LANES),
+            f32(count, LANES), f32(1, LANES), i32(1, slabs * CAP), i32(*new_source.shape),
+            i32(*cell_block.shape), f32(1, count), f32(1, count), f32(old_slots, count, cells),
+            *(plane,) * 7, edge, edge,
         ),
         [HBM] * 9,
-        (VMEM,) * 18,
+        (VMEM,) * 17,
         tuple(
             pltpu.with_memory_space_constraint(value, pltpu.HBM)
             for value in (
@@ -437,8 +482,6 @@
         ),
         [
             pltpu.VMEM((3, width // LANES, height, LANES), jnp.float32),
-            pltpu.VMEM(new_source.shape, jnp.int32),
-            pltpu.VMEM(cell_block.shape, jnp.int32),
             pltpu.SMEM(cell_block.shape, jnp.int32),
             pltpu.SemaphoreType.DMA((9,)),
             pltpu.SemaphoreType.DMA((4,)),
@@ -454,7 +497,16 @@
         (VMEM,) * chips,
         (slot, held, hopped),
     )
-    side = call(side_kernel, f32(tall, LANES), [VMEM] * 3, VMEM, (side, edge_a, edge_b))
+    side, place, recv = call(
+        side_kernel,
+        (f32(tall, LANES), i32(1, slabs * CAP), i32(1, new_slots)),
+        [VMEM] * 11,
+        (VMEM,) * 3,
+        (
+            table, block_row, pressure, storage, trans, source, base1, base2, coef,
+            edge_a, edge_b,
+        ),
+    )
     side_c = lax.ppermute(side, "col", swaps(cols, False))
     side_d = lax.ppermute(side, "col", swaps(cols, True)) if cols > 2 else side_c
     blocks = {0: packed[0]}
@@ -464,13 +516,17 @@
     result, rows = call(
         fracture_kernel,
         (plane, f32(slabs, tail, LANES)),
-        [SMEM] + [VMEM] * 12,
+        [VMEM] * 13,
         (VMEM, VMEM),
         (
             place, const, pressure, storage, trans, source, base1, base2, coef,
             edge_a, edge_b, side_c, side_d,
         ),
-        [pltpu.VMEM((STEPS, width // LANES, height, LANES), jnp.float32)],
+        [
+            pltpu.VMEM((STEPS, width // LANES, height, LANES), jnp.float32),
+            pltpu.SMEM(place.shape, jnp.int32),
+            pltpu.SemaphoreType.DMA,
+        ],
     )
     other_rows = lax.ppermute(rows, "slab", swaps(slabs, False))
     local_rows, *filled = call(
@@ -486,17 +542,35 @@
     for k, value in zip(late_k, filled):
         blocks[k] = chip_swap(value, k)
     loose = [chip_swap(value, k) for k, value in zip(early_k, filled[len(late_k) :])]
+    ready_k = [k for k in range(chips) if k not in late_k]
+    left, coefficients, product = call(
+        product_kernel,
+        (
+            jax.ShapeDtypeStruct((count, 3 * count), jnp.bfloat16),
+            f32(2, count, LANES),
+            f32(len(ready_k) * CAP, count, cells),
+        ),
+        [VMEM] * (3 + len(ready_k)),
+        (VMEM,) * 3,
+        (cap_row, trans_row, inverse, *(blocks[k] for k in ready_k)),
+    )
+    loose_k = [0, *early_k]
     shells_new = call(
-        final_kernel,
+        functools.partial(final_kernel, ready_k, late_k, loose_k),
         f32(new_slots, count, cells),
-        [SMEM] + [VMEM] * (3 + chips + 1 + len(early_k)),
+        [VMEM] * (4 + chips),
         ANY,
-        (recv, cap_row, trans_row, inverse, *(blocks[k] for k in range(chips)), local_rows, *loose),
+        (
+            recv, left, coefficients, product,
+            *(blocks[k] for k in late_k), local_rows, *loose,
+        ),
         [
             pltpu.VMEM((chips * CAP, count, cells), jnp.float32),
             pltpu.VMEM((chips, tail, cells), jnp.float32),
             pltpu.VMEM((new_slots, count, cells), jnp.float32),
-            pltpu.SemaphoreType.DMA((new_slots // 2,)),
+            pltpu.SMEM(recv.shape, jnp.int32),
+            pltpu.SemaphoreType.DMA,
+            pltpu.SemaphoreType.DMA((new_slots // 4,)),
         ],
     )
     return (result, shells_new[None])

time: 47.1 us -> 50.5 us (1.072)
  the two profiles are of different devices: /device:TPU:16 before, /device:TPU:0 now
where the time goes in v2:
time: 50.5 us; the launch traced here: 50.3 us
  starting transfers between devices  21.5 us (43%)
  waiting for transfers between devices  20.1 us (40%)
  Pallas kernels  7.93 us (16%)
  between operations  0.71 us (1%)
    ppermute x10, starting transfers between devices, chip_swap(): return lax.ppermute(value, 'slab', [(i, i ^ 2 * k) for i in range(slabs)])  17.1 us
    ppermute x10, waiting for transfers between devices, chip_swap(): return lax.ppermute(value, 'slab', [(i, i ^ 2 * k) for i in range(slabs)])  14 us
    pallas_call x7, Pallas kernels, call(): pl.pallas_call(kernel, out_shape=out_shape, in_specs=in_specs, out_specs=...  7.93 us
    ppermute x1, waiting for transfers between devices, shards(): side_c = lax.ppermute(side, 'col', swaps(cols, False))  2.48 us
    ppermute x1, waiting for transfers between devices, shards(): edge_b = lax.ppermute(edge_b, 'slab', shifts(slabs))  2.44 us
    ppermute x1, starting transfers between devices, shards(): edge_a = lax.ppermute(edge_a, 'slab', swaps(slabs, False))  2.21 us
    ppermute x1, starting transfers between devices, shards(): side_c = lax.ppermute(side, 'col', swaps(cols, False))  1.58 us
    ppermute x1, waiting for transfers between devices, shards(): other_rows = lax.ppermute(rows, 'slab', swaps(slabs, False))  1.24 us
  transfers between devices with their start and end apart: 16, of which 7 were waited for; matrix products, arithmetic and copies ran while one was open for 0% of the time, Pallas kernels for 13%

profile of v2, /device:TPU:0, one launch (start us, length us, event | category | flops | bytes accessed | tf_op | source)
XLA Modules:
  0.0 50.3 jit_solution(11714717990335412916)
XLA Ops:
  0.6 0.6 %collective-permute-start.4 = (f32[64,64,128]{2,1,0:T(8,128)}, f32[64,64,128]{2,1,0:T(8,128)S(1)}, u32[]{:S(2)}, u32[]{:S(2)}) collective-permute-start(f32[64,64,128]{2,1,0:T(8,128)} %bitcast.4), channel_id=1, source_target_pairs={{0,2},{2,0},{4,6},{6,4},{8,10},{10,8},{12,14},{14,12},{16,18},{18,... | collective-permute-start | bytes 6291464 | tf_op jit(solution)/shard_map/ppermute | solution.py:463
  1.2 2.5 %shard_map.104 = (f32[64,128]{1,0:T(8,128)S(1)}, f32[1,128]{1,0:T(1,128)S(1)}, s32[1,64]{1,0:T(1,128)S(1)}, s32[1,512]{1,0:T(1,128)S(1)}, s32[1,64]{1,0:T(1,128)...) custom-call(f32[1,64]{1,0:T(1,128)} %bitcast.7, ...), custom_call_target="tpu_custom_call" | custom-call | tf_op jit(solution)/shard_map/pallas_call | solution.py:407
  3.7 0.1 collective-permute-start.1
  3.8 2.2 %collective-permute-start = (f32[7,8,256]{2,1,0:T(8,128)S(1)}, f32[7,8,256]{2,1,0:T(8,128)S(1)}, u32[]{:S(2)}, u32[]{:S(2)}) collective-permute-start(f32[7,8,256]{2,1,0:T(8,128)S(1)} %get-tuple-element.52), channel_id=1, source_target_pairs={{0,2},{2,0},{4,6},{6,4},{8,10},{10,8},{12,14},{14,12},{16,18},{18,... | collective-permute-start | bytes 172040 | tf_op jit(solution)/shard_map/ppermute | solution.py:492
  6.0 2.4 %collective-permute-done.1 = f32[7,8,256]{2,1,0:T(8,128)S(1)} collective-permute-done((f32[7,8,256]{2,1,0:T(8,128)S(1)}, f32[7,8,256]{2,1,0:T(8,128)S(1)}, u32[]{:S(2)}, u32[]{:S(2)}) %collective-permute-start.1) | collective-permute-done | bytes 57376 | tf_op jit(solution)/shard_map/ppermute | solution.py:490
  8.4 0.0 collective-permute-start.2
  8.4 0.0 collective-permute-done.4.other_ref
  8.4 0.6 %shard_map.107 = (f32[4,64,128]{2,1,0:T(8,128)S(1)}, f32[4,72,128]{2,1,0:T(8,128)S(1)}, f32[4,72,128]{2,1,0:T(8,128)S(1)}, f32[4,72,128]{2,1,0:T(8,128)S(1)}, f3...) custom-call(s32[1,64]{1,0:T(1,128)S(1)} %get-tuple-element.62.slot_r, ...), custom_call_target="tpu_custom_call" | custom-call | tf_op jit(solution)/shard_map/pallas_call | solution.py:407
  9.1 3.7 %collective-permute-start.5 = (f32[4,64,128]{2,1,0:T(8,128)S(1)}, f32[4,64,128]{2,1,0:T(8,128)S(1)}, u32[]{:S(2)}, u32[]{:S(2)}) collective-permute-start(f32[4,64,128]{2,1,0:T(8,128)S(1)} %get-tuple-element.65), channel_id=1, source_target_pairs={{0,16},{2,18},{4,20},{6,22},{8,24},{10,26},{12,28},{14,30},{16,0},... | collective-permute-start | bytes 393224 | tf_op jit(solution)/shard_map/ppermute | solution.py:461
  12.8 1.6 %collective-permute-start.6 = (f32[4,64,128]{2,1,0:T(8,128)S(1)}, f32[4,64,128]{2,1,0:T(8,128)S(1)}, u32[]{:S(2)}, u32[]{:S(2)}) collective-permute-start(f32[4,64,128]{2,1,0:T(8,128)S(1)} %get-tuple-element.66), channel_id=1, source_target_pairs={{0,20},{2,22},{4,16},{6,18},{8,28},{10,30},{12,24},{14,26},{16,4},... | collective-permute-start | bytes 393224 | tf_op jit(solution)/shard_map/ppermute | solution.py:461
  14.4 0.0 collective-permute-done.rest_7_.a_ref
  14.4 0.0 collective-permute-done.2.rest_8_.b_ref
  14.4 0.6 %shard_map.105 = (f32[80,128]{1,0:T(8,128)S(1)}, s32[1,64]{1,0:T(1,128)S(1)}, s32[1,32]{1,0:T(1,128)S(1)}) custom-call(s32[1,512]{1,0:T(1,128)S(1)} %get-tuple-element.43.table_ref, s32[1,64]{1,0:T(1,128)S(1)} %get-tuple-element.44.block_ref, f32[64,256]{1,0:T(8,128)S(1)} %get-tuple-element.45.rest_0_.p_ref, ...), custom_call_target="tpu_custom_call" | custom-call | tf_op jit(solution)/shard_map/pallas_call | solution.py:407
  15.0 1.6 %collective-permute-start.3 = (f32[80,128]{1,0:T(8,128)S(1)}, f32[80,128]{1,0:T(8,128)S(1)}, u32[]{:S(2)}, u32[]{:S(2)}) collective-permute-start(f32[80,128]{1,0:T(8,128)S(1)} %get-tuple-element.56), channel_id=1, source_target_pairs={{0,1},{1,0},{2,3},{3,2},{4,5},{5,4},{6,7},{7,6},{8,9},{9,8},{10,11... | collective-permute-start | bytes 122888 | tf_op jit(solution)/shard_map/ppermute | solution.py:510
  16.6 2.5 %collective-permute-done.3.c_ref.d_ref = f32[80,128]{1,0:T(8,128)S(1)} collective-permute-done((f32[80,128]{1,0:T(8,128)S(1)}, f32[80,128]{1,0:T(8,128)S(1)}, u32[]{:S(2)}, u32[]{:S(2)}) %collective-permute-start.3) | collective-permute-done | bytes 40992 | tf_op jit(solution)/shard_map/ppermute | solution.py:510
  19.1 2.1 %shard_map.106 = (f32[64,256]{1,0:T(8,128)}, f32[16,8,128]{2,1,0:T(8,128)S(1)}) custom-call(s32[1,64]{1,0:T(1,128)S(1)} %get-tuple-element.54.place_ref, f32[1,128]{1,0:T(1,128)S(1)} %get-tuple-element.55.const_ref, f32[64,256]{1,0:T(8,128)S(1)} %get-tuple-element.45.rest_0_.p_ref, f32[64,256]{1,0:T(8,128)S(1)} %get-tuple-element.46.rest_1_.storage_ref, ...), custom_call_target="tpu_custom_call" | custom-call | tf_op jit(solution)/shard_map/pallas_call | solution.py:407
  21.2 0.1 collective-permute-start.8
  21.3 1.2 %collective-permute-done.8.other_ref = f32[16,8,128]{2,1,0:T(8,128)S(1)} collective-permute-done((f32[16,8,128]{2,1,0:T(8,128)S(1)}, f32[16,8,128]{2,1,0:T(8,128)S(1)}, u32[]{:S(2)}, u32[]{:S(2)}) %collective-permute-start.8) | collective-permute-done | bytes 65568 | tf_op jit(solution)/shard_map/ppermute | solution.py:531
  22.5 2.7 %collective-permute-start.13 = (f32[8,128]{1,0:T(8,128)S(1)}, f32[8,128]{1,0:T(8,128)S(1)}, u32[]{:S(2)}, u32[]{:S(2)}) collective-permute-start(f32[8,128]{1,0:T(8,128)S(1)} %get-tuple-element.81), channel_id=1, source_target_pairs={{0,16},{2,18},{4,20},{6,22},{8,24},{10,26},{12,28},{14,30},{16,0},... | collective-permute-start | bytes 12296 | tf_op jit(solution)/shard_map/ppermute | solution.py:461
  25.2 0.0 collective-permute-start.14
  25.2 1.8 %collective-permute-start.9 = (f32[4,72,128]{2,1,0:T(8,128)S(1)}, f32[4,72,128]{2,1,0:T(8,128)S(1)}, u32[]{:S(2)}, u32[]{:S(2)}) collective-permute-start(f32[4,72,128]{2,1,0:T(8,128)S(1)} %get-tuple-element.76), channel_id=1, source_target_pairs={{0,4},{2,6},{4,0},{6,2},{8,12},{10,14},{12,8},{14,10},{16,20},{18,... | collective-permute-start | bytes 442376 | tf_op jit(solution)/shard_map/ppermute | solution.py:461
  27.0 0.1 collective-permute-done.13.rest_5_
  27.1 1.6 %collective-permute-start.10 = (f32[4,72,128]{2,1,0:T(8,128)S(1)}, f32[4,72,128]{2,1,0:T(8,128)S(1)}, u32[]{:S(2)}, u32[]{:S(2)}) collective-permute-start(f32[4,72,128]{2,1,0:T(8,128)S(1)} %get-tuple-element.77), channel_id=1, source_target_pairs={{0,8},{2,10},{4,12},{6,14},{8,0},{10,2},{12,4},{14,6},{16,24},{18,... | collective-permute-start | bytes 442376 | tf_op jit(solution)/shard_map/ppermute | solution.py:461
  28.7 2.0 %collective-permute-done.14.rest_6_ = f32[8,128]{1,0:T(8,128)S(1)} collective-permute-done((f32[8,128]{1,0:T(8,128)S(1)}, f32[8,128]{1,0:T(8,128)S(1)}, u32[]{:S(2)}, u32[]{:S(2)}) %collective-permute-start.14) | collective-permute-done | bytes 4128 | tf_op jit(solution)/shard_map/ppermute | solution.py:461
  30.7 1.2 %collective-permute-start.11 = (f32[4,72,128]{2,1,0:T(8,128)S(1)}, f32[4,72,128]{2,1,0:T(8,128)S(1)}, u32[]{:S(2)}, u32[]{:S(2)}) collective-permute-start(f32[4,72,128]{2,1,0:T(8,128)S(1)} %get-tuple-element.78), channel_id=1, source_target_pairs={{0,12},{2,14},{4,8},{6,10},{8,4},{10,6},{12,0},{14,2},{16,28},{18,... | collective-permute-start | bytes 442376 | tf_op jit(solution)/shard_map/ppermute | solution.py:461
  31.9 0.0 collective-permute-done.5.rest_1_
  31.9 1.5 %collective-permute-start.12 = (f32[4,72,128]{2,1,0:T(8,128)S(1)}, f32[4,72,128]{2,1,0:T(8,128)S(1)}, u32[]{:S(2)}, u32[]{:S(2)}) collective-permute-start(f32[4,72,128]{2,1,0:T(8,128)S(1)} %get-tuple-element.79), channel_id=1, source_target_pairs={{0,28},{2,30},{4,24},{6,26},{8,20},{10,22},{12,16},{14,18},{16,12}... | collective-permute-start | bytes 442376 | tf_op jit(solution)/shard_map/ppermute | solution.py:461
  33.4 0.0 collective-permute-done.6.rest_2_
  33.4 1.6 %collective-permute-start.7 = (f32[4,64,128]{2,1,0:T(8,128)S(1)}, f32[4,64,128]{2,1,0:T(8,128)S(1)}, u32[]{:S(2)}, u32[]{:S(2)}) collective-permute-start(f32[4,64,128]{2,1,0:T(8,128)S(1)} %get-tuple-element.67), channel_id=1, source_target_pairs={{0,24},{2,26},{4,28},{6,30},{8,16},{10,18},{12,20},{14,22},{16,8},... | collective-permute-start | bytes 393224 | tf_op jit(solution)/shard_map/ppermute | solution.py:461
  34.9 8.4 %collective-permute-done.7.rest_3_ = f32[4,64,128]{2,1,0:T(8,128)S(1)} collective-permute-done((f32[4,64,128]{2,1,0:T(8,128)S(1)}, f32[4,64,128]{2,1,0:T(8,128)S(1)}, u32[]{:S(2)}, u32[]{:S(2)}) %collective-permute-start.7) | collective-permute-done | bytes 131104 | tf_op jit(solution)/shard_map/ppermute | solution.py:461
  43.3 1.4 %collective-permute-start.15 = (f32[8,128]{1,0:T(8,128)S(1)}, f32[8,128]{1,0:T(8,128)S(1)}, u32[]{:S(2)}, u32[]{:S(2)}) collective-permute-start(f32[8,128]{1,0:T(8,128)S(1)} %get-tuple-element.83), channel_id=1, source_target_pairs={{0,24},{2,26},{4,28},{6,30},{8,16},{10,18},{12,20},{14,22},{16,8},... | collective-permute-start | bytes 12296 | tf_op jit(solution)/shard_map/ppermute | solution.py:461
  44.7 0.5 shard_map.108
  45.2 3.5 %collective-permute-done.15.rest_7_ = f32[8,128]{1,0:T(8,128)S(1)} collective-permute-done((f32[8,128]{1,0:T(8,128)S(1)}, f32[8,128]{1,0:T(8,128)S(1)}, u32[]{:S(2)}, u32[]{:S(2)}) %collective-permute-start.15) | collective-permute-done | bytes 4128 | tf_op jit(solution)/shard_map/ppermute | solution.py:461
  48.7 0.0 collective-permute-done.9.rest_0_
  48.7 0.0 collective-permute-done.10.rest_1_
  48.7 0.0 collective-permute-done.11.rest_2_
  48.7 0.0 collective-permute-done.12.rest_3_
  48.7 1.6 %shard_map.110 = f32[32,64,128]{2,1,0:T(8,128)} custom-call(s32[1,32]{1,0:T(1,128)S(1)} %get-tuple-element.58.recv_ref, bf16[64,192]{1,0:T(8,128)(2,1)S(1)} %get-tuple-element.68.left_ref, f32[2,64,128]{2,1,0:T(8,128)S(1)} %get-tuple-element.69.m_ref, f32[16,64,128]{2,1,0:T(8,128)S(1)} %get-tuple-element.70.product_ref, ...), custom_call_target="tpu_custom_call" | custom-call | tf_op jit(solution)/shard_map/pallas_call | solution.py:407
  (1 shorter events, 0.0 us)
Async XLA Ops:
  0.6 7.8 %collective-permute-start.4 = (f32[64,64,128]{2,1,0:T(8,128)}, f32[64,64,128]{2,1,0:T(8,128)S(1)}, u32[]{:S(2)}, u32[]{:S(2)}) collective-permute-start(f32[64,64,128]{2,1,0:T(8,128)} %bitcast.4), channel_id=1, source_target_pairs={{0,2},{2,0},{4,6},{6,4},{8,10},{10,8},{12,14},{14,12},{16,18},{18,... | collective-permute-start | bytes 6291464 | tf_op jit(solution)/shard_map/ppermute | solution.py:463
  3.7 4.7 %collective-permute-start.1 = (f32[7,8,256]{2,1,0:T(8,128)S(1)}, f32[7,8,256]{2,1,0:T(8,128)S(1)}, u32[]{:S(2)}, u32[]{:S(2)}) collective-permute-start(f32[7,8,256]{2,1,0:T(8,128)S(1)} %get-tuple-element.53), channel_id=1, source_target_pairs={{0,2},{2,6},{4,0},{6,10},{8,4},{10,14},{12,8},{14,18},{16,12},{18,... | collective-permute-start | bytes 172040 | tf_op jit(solution)/shard_map/ppermute | solution.py:490
  3.8 10.6 %collective-permute-start = (f32[7,8,256]{2,1,0:T(8,128)S(1)}, f32[7,8,256]{2,1,0:T(8,128)S(1)}, u32[]{:S(2)}, u32[]{:S(2)}) collective-permute-start(f32[7,8,256]{2,1,0:T(8,128)S(1)} %get-tuple-element.52), channel_id=1, source_target_pairs={{0,2},{2,0},{4,6},{6,4},{8,10},{10,8},{12,14},{14,12},{16,18},{18,... | collective-permute-start | bytes 172040 | tf_op jit(solution)/shard_map/ppermute | solution.py:492
  8.4 6.0 %collective-permute-start.2 = (f32[7,8,256]{2,1,0:T(8,128)S(1)}, f32[7,8,256]{2,1,0:T(8,128)S(1)}, u32[]{:S(2)}, u32[]{:S(2)}) collective-permute-start(f32[7,8,256]{2,1,0:T(8,128)S(1)} %collective-permute-done.1), channel_id=1, source_target_pairs={{0,2},{2,0},{4,6},{6,4},{8,10},{10,8},{12,14},{14,12},{16,18},{18,... | collective-permute-start | bytes 172040 | tf_op jit(solution)/shard_map/ppermute | solution.py:491
  9.1 22.8 %collective-permute-start.5 = (f32[4,64,128]{2,1,0:T(8,128)S(1)}, f32[4,64,128]{2,1,0:T(8,128)S(1)}, u32[]{:S(2)}, u32[]{:S(2)}) collective-permute-start(f32[4,64,128]{2,1,0:T(8,128)S(1)} %get-tuple-element.65), channel_id=1, source_target_pairs={{0,16},{2,18},{4,20},{6,22},{8,24},{10,26},{12,28},{14,30},{16,0},... | collective-permute-start | bytes 393224 | tf_op jit(solution)/shard_map/ppermute | solution.py:461
  12.8 20.6 %collective-permute-start.6 = (f32[4,64,128]{2,1,0:T(8,128)S(1)}, f32[4,64,128]{2,1,0:T(8,128)S(1)}, u32[]{:S(2)}, u32[]{:S(2)}) collective-permute-start(f32[4,64,128]{2,1,0:T(8,128)S(1)} %get-tuple-element.66), channel_id=1, source_target_pairs={{0,20},{2,22},{4,16},{6,18},{8,28},{10,30},{12,24},{14,26},{16,4},... | collective-permute-start | bytes 393224 | tf_op jit(solution)/shard_map/ppermute | solution.py:461
  15.0 4.1 %collective-permute-start.3 = (f32[80,128]{1,0:T(8,128)S(1)}, f32[80,128]{1,0:T(8,128)S(1)}, u32[]{:S(2)}, u32[]{:S(2)}) collective-permute-start(f32[80,128]{1,0:T(8,128)S(1)} %get-tuple-element.56), channel_id=1, source_target_pairs={{0,1},{1,0},{2,3},{3,2},{4,5},{5,4},{6,7},{7,6},{8,9},{9,8},{10,11... | collective-permute-start | bytes 122888 | tf_op jit(solution)/shard_map/ppermute | solution.py:510
  21.2 1.3 %collective-permute-start.8 = (f32[16,8,128]{2,1,0:T(8,128)S(1)}, f32[16,8,128]{2,1,0:T(8,128)S(1)}, u32[]{:S(2)}, u32[]{:S(2)}) collective-permute-start(f32[16,8,128]{2,1,0:T(8,128)S(1)} %get-tuple-element.71.own_ref), channel_id=1, source_target_pairs={{0,2},{2,0},{4,6},{6,4},{8,10},{10,8},{12,14},{14,12},{16,18},{18,... | collective-permute-start | bytes 196616 | tf_op jit(solution)/shard_map/ppermute | solution.py:531
  22.5 4.6 %collective-permute-start.13 = (f32[8,128]{1,0:T(8,128)S(1)}, f32[8,128]{1,0:T(8,128)S(1)}, u32[]{:S(2)}, u32[]{:S(2)}) collective-permute-start(f32[8,128]{1,0:T(8,128)S(1)} %get-tuple-element.81), channel_id=1, source_target_pairs={{0,16},{2,18},{4,20},{6,22},{8,24},{10,26},{12,28},{14,30},{16,0},... | collective-permute-start | bytes 12296 | tf_op jit(solution)/shard_map/ppermute | solution.py:461
  25.2 5.5 %collective-permute-start.14 = (f32[8,128]{1,0:T(8,128)S(1)}, f32[8,128]{1,0:T(8,128)S(1)}, u32[]{:S(2)}, u32[]{:S(2)}) collective-permute-start(f32[8,128]{1,0:T(8,128)S(1)} %get-tuple-element.82), channel_id=1, source_target_pairs={{0,20},{2,22},{4,16},{6,18},{8,28},{10,30},{12,24},{14,26},{16,4},... | collective-permute-start | bytes 12296 | tf_op jit(solution)/shard_map/ppermute | solution.py:461
  25.2 23.5 %collective-permute-start.9 = (f32[4,72,128]{2,1,0:T(8,128)S(1)}, f32[4,72,128]{2,1,0:T(8,128)S(1)}, u32[]{:S(2)}, u32[]{:S(2)}) collective-permute-start(f32[4,72,128]{2,1,0:T(8,128)S(1)} %get-tuple-element.76), channel_id=1, source_target_pairs={{0,4},{2,6},{4,0},{6,2},{8,12},{10,14},{12,8},{14,10},{16,20},{18,... | collective-permute-start | bytes 442376 | tf_op jit(solution)/shard_map/ppermute | solution.py:461
  27.1 21.6 %collective-permute-start.10 = (f32[4,72,128]{2,1,0:T(8,128)S(1)}, f32[4,72,128]{2,1,0:T(8,128)S(1)}, u32[]{:S(2)}, u32[]{:S(2)}) collective-permute-start(f32[4,72,128]{2,1,0:T(8,128)S(1)} %get-tuple-element.77), channel_id=1, source_target_pairs={{0,8},{2,10},{4,12},{6,14},{8,0},{10,2},{12,4},{14,6},{16,24},{18,... | collective-permute-start | bytes 442376 | tf_op jit(solution)/shard_map/ppermute | solution.py:461
  30.7 18.0 %collective-permute-start.11 = (f32[4,72,128]{2,1,0:T(8,128)S(1)}, f32[4,72,128]{2,1,0:T(8,128)S(1)}, u32[]{:S(2)}, u32[]{:S(2)}) collective-permute-start(f32[4,72,128]{2,1,0:T(8,128)S(1)} %get-tuple-element.78), channel_id=1, source_target_pairs={{0,12},{2,14},{4,8},{6,10},{8,4},{10,6},{12,0},{14,2},{16,28},{18,... | collective-permute-start | bytes 442376 | tf_op jit(solution)/shard_map/ppermute | solution.py:461
  31.9 16.8 %collective-permute-start.12 = (f32[4,72,128]{2,1,0:T(8,128)S(1)}, f32[4,72,128]{2,1,0:T(8,128)S(1)}, u32[]{:S(2)}, u32[]{:S(2)}) collective-permute-start(f32[4,72,128]{2,1,0:T(8,128)S(1)} %get-tuple-element.79), channel_id=1, source_target_pairs={{0,28},{2,30},{4,24},{6,26},{8,20},{10,22},{12,16},{14,18},{16,12}... | collective-permute-start | bytes 442376 | tf_op jit(solution)/shard_map/ppermute | solution.py:461
  33.4 9.9 %collective-permute-start.7 = (f32[4,64,128]{2,1,0:T(8,128)S(1)}, f32[4,64,128]{2,1,0:T(8,128)S(1)}, u32[]{:S(2)}, u32[]{:S(2)}) collective-permute-start(f32[4,64,128]{2,1,0:T(8,128)S(1)} %get-tuple-element.67), channel_id=1, source_target_pairs={{0,24},{2,26},{4,28},{6,30},{8,16},{10,18},{12,20},{14,22},{16,8},... | collective-permute-start | bytes 393224 | tf_op jit(solution)/shard_map/ppermute | solution.py:461
  43.3 5.4 %collective-permute-start.15 = (f32[8,128]{1,0:T(8,128)S(1)}, f32[8,128]{1,0:T(8,128)S(1)}, u32[]{:S(2)}, u32[]{:S(2)}) collective-permute-start(f32[8,128]{1,0:T(8,128)S(1)} %get-tuple-element.83), channel_id=1, source_target_pairs={{0,24},{2,26},{4,28},{6,30},{8,16},{10,18},{12,20},{14,22},{16,8},... | collective-permute-start | bytes 12296 | tf_op jit(solution)/shard_map/ppermute | solution.py:461

commit v3 on v2

--- a/solution.py
+++ b/solution.py
@@ -66,8 +66,9 @@
     while step < count:
         down = functools.partial(pltpu.roll, shift=step, axis=0)
         up = functools.partial(pltpu.roll, shift=count - step, axis=0)
-        alpha = low / down(diag)
-        gamma = high / up(diag)
+        once = 1.0 / diag
+        alpha = low * down(once)
+        gamma = high * up(once)
         diag = diag - alpha * down(high) - gamma * up(low)
         rhs = rhs + alpha * down(rhs) + gamma * up(rhs)
         low, high = alpha * down(low), gamma * up(high)
@@ -87,7 +88,7 @@
     while shift < new_slots:
         seen = seen + jnp.where(within >= shift, pltpu.roll(seen, shift, axis=1), 0)
         shift *= 2
-    return jnp.where(mine, dest * CAP + jnp.minimum(seen, CAP) - 1, -1), local
+    return mine, dest, jnp.minimum(seen, CAP) - 1, local
 
 
 def pack_sides(get, rows):
@@ -106,9 +107,9 @@
 
 def base_kernel(
     cap_hbm, trans_hbm, table_hbm, block_hbm, shells_hbm, p_hbm, storage_hbm, t_hbm, source_hbm,
-    inv_ref, const_ref, slot_ref, table_ref, block_row, cap_ref, trans_ref, held,
+    inv_ref, const_ref, slot_ref, place_ref, recv_ref, cap_ref, trans_ref, held,
     p_ref, storage_ref, t_ref, source_ref, b1_ref, b2_ref, e_ref, a_ref, b_ref,
-    tiles, block_ref, sem, chunk_sem,
+    tiles, table_ref, block_row, block_ref, sem, chunk_sem,
 ):
     me = lax.axis_index("slab")
     slabs = lax.axis_size("slab")
@@ -178,65 +179,17 @@
         top, bottom = ref[0:EDGE, :], ref[height - EDGE : height, :]
         a_ref[f] = jnp.where(even, bottom, top)
         b_ref[f] = jnp.where(even, top, bottom)
-    target, local = sent_blocks(table_ref[...], old_slots, slabs)
-    slot_ref[...] = placed(target, local, slabs * CAP)
-
-
-def pack_kernel(slot_ref, own_ref, other_ref, *out_refs):
-    me = lax.axis_index("slab")
-    chip, core = me // 2, me % 2
-    count = own_ref.shape[1]
-
-    def fill(source):
-        for k, ref in enumerate(out_refs):
-            for r in range(CAP):
-                ref[r, :count] = source[slot_ref[0, ((chip ^ k) * 2 + core) * CAP + r]]
-
-    @pl.when(core == 0)
-    def _():
-        fill(own_ref)
-
-    @pl.when(core == 1)
-    def _():
-        fill(other_ref)
-
-
-def rows_kernel(late_k, early_k, own_ref, other_ref, *rest):
-    local_ref, *outs = rest[len(late_k) :]
-    me = lax.axis_index("slab")
-
-    def rows(k):
-        at = ((me // 2) ^ k) * 2 + me % 2
-        return jnp.where(me % 2 == 0, own_ref[at], other_ref[at])
-
-    local_ref[...] = rows(0)
-    for k, ref in zip(late_k, outs):
-        value = rows(k)
-        ref[0, ref.shape[1] - value.shape[0] :] = value
-    for k, ref in zip(early_k, outs[len(late_k) :]):
-        ref[...] = rows(k)
-
-
-def side_kernel(table_ref, block_ref, *rest):
-    *fields, a_ref, b_ref, out_ref, place_ref, recv_ref = rest
-    me, slabs = lax.axis_index("slab"), lax.axis_size("slab")
-    even = me % 2 == 0
-    height = fields[0].shape[0]
-    from_a = pack_sides(lambda f: a_ref[f], EDGE)
-    from_b = pack_sides(lambda f: b_ref[f], EDGE)
-    out_ref[0:EDGE] = jnp.where(even, from_b, from_a)
-    out_ref[EDGE : EDGE + height] = pack_sides(lambda f: fields[f][...], height)
-    out_ref[EDGE + height :] = jnp.where(even, from_a, from_b)
-
-    old_slots = block_ref.shape[1]
     table = table_ref[...]
     total = table.shape[1]
-    target, local = sent_blocks(table, old_slots, slabs)
+    mine, dest, rank, local = sent_blocks(table, old_slots, slabs)
+    distance = (dest >> 1) ^ (me // 2)
+    here = mine & ((dest & 1) == me % 2)
+    slot_ref[...] = placed(jnp.where(here, distance * CAP + rank, -1), local, slot_ref.shape[1])
     eye = iota((old_slots, old_slots), 0) == iota((old_slots, old_slots), 1)
-    column = column_of(block_ref[...].astype(jnp.float32), eye)
+    column = column_of(block_row[...].astype(jnp.float32), eye)
     owner = iota((old_slots, total), 0) == local
-    here = jnp.sum(jnp.where(owner, column, 0.0), axis=0, keepdims=True)
-    place_ref[...] = placed(target, here, slabs * CAP)
+    block = jnp.sum(jnp.where(owner, column, 0.0), axis=0, keepdims=True)
+    place_ref[...] = placed(jnp.where(mine, dest * CAP + rank, -1), block, slabs * CAP)
 
     count = recv_ref.shape[1]
     anchor, _ = split_by(placed(iota((1, total), 1) - me * count, table, count), old_slots)
@@ -246,6 +199,51 @@
     rank = row_of(jnp.sum(jnp.where(same, 1.0, 0.0), axis=1, keepdims=True), count)
     rank = jnp.minimum(rank.astype(jnp.int32), CAP - 1)
     recv_ref[...] = ((anchor >> 1) ^ (me // 2)) * CAP + rank
+
+
+def pack_kernel(slot_ref, own_ref, other_ref, *out_refs):
+    core = lax.axis_index("slab") % 2
+    count = own_ref.shape[1]
+
+    def fill(source):
+        for k, ref in enumerate(out_refs):
+            for r in range(CAP):
+                ref[r, :count] = source[slot_ref[0, k * CAP + r]]
+
+    @pl.when(core == 0)
+    def _():
+        fill(own_ref)
+
+    @pl.when(core == 1)
+    def _():
+        fill(other_ref)
+
+
+def rows_kernel(late_k, early_k, own_ref, other_ref, *rest):
+    local_ref, *outs = rest[len(late_k) :]
+    me = lax.axis_index("slab")
+
+    def rows(k):
+        at = ((me // 2) ^ k) * 2 + me % 2
+        return jnp.where(me % 2 == 0, own_ref[at], other_ref[at])
+
+    local_ref[...] = rows(0)
+    for k, ref in zip(late_k, outs):
+        value = rows(k)
+        ref[0, ref.shape[1] - value.shape[0] :] = value
+    for k, ref in zip(early_k, outs[len(late_k) :]):
+        ref[...] = rows(k)
+
+
+def side_kernel(*refs):
+    *fields, a_ref, b_ref, out_ref = refs
+    even = lax.axis_index("slab") % 2 == 0
+    height = fields[0].shape[0]
+    from_a = pack_sides(lambda f: a_ref[f], EDGE)
+    from_b = pack_sides(lambda f: b_ref[f], EDGE)
+    out_ref[0:EDGE] = jnp.where(even, from_b, from_a)
+    out_ref[EDGE : EDGE + height] = pack_sides(lambda f: fields[f][...], height)
+    out_ref[EDGE + height :] = jnp.where(even, from_a, from_b)
 
 
 def fracture_kernel(
@@ -463,13 +461,13 @@
     hopped = lax.ppermute(shells, "slab", swaps(slabs, False))
     plane, edge = f32(height, width), f32(FIELDS, EDGE, width)
     (
-        inverse, const, slot, table, block_row, cap_row, trans_row, held,
+        inverse, const, slot, place, recv, cap_row, trans_row, held,
         pressure, storage, trans, source, base1, base2, coef, edge_a, edge_b,
     ) = call(
         base_kernel,
         (
-            f32(count, LANES), f32(1, LANES), i32(1, slabs * CAP), i32(*new_source.shape),
-            i32(*cell_block.shape), f32(1, count), f32(1, count), f32(old_slots, count, cells),
+            f32(count, LANES), f32(1, LANES), i32(1, chips * CAP), i32(1, slabs * CAP),
+            i32(1, new_slots), f32(1, count), f32(1, count), f32(old_slots, count, cells),
             *(plane,) * 7, edge, edge,
         ),
         [HBM] * 9,
@@ -482,6 +480,8 @@
         ),
         [
             pltpu.VMEM((3, width // LANES, height, LANES), jnp.float32),
+            pltpu.VMEM(new_source.shape, jnp.int32),
+            pltpu.VMEM(cell_block.shape, jnp.int32),
             pltpu.SMEM(cell_block.shape, jnp.int32),
             pltpu.SemaphoreType.DMA((9,)),
             pltpu.SemaphoreType.DMA((4,)),
@@ -493,19 +493,16 @@
     packed = call(
         pack_kernel,
         tuple(f32(CAP, count + (tail if k in late_k else 0), cells) for k in range(chips)),
-        [SMEM, VMEM, VMEM],
+        [VMEM, VMEM, VMEM],
         (VMEM,) * chips,
         (slot, held, hopped),
     )
-    side, place, recv = call(
+    side = call(
         side_kernel,
-        (f32(tall, LANES), i32(1, slabs * CAP), i32(1, new_slots)),
-        [VMEM] * 11,
-        (VMEM,) * 3,
-        (
-            table, block_row, pressure, storage, trans, source, base1, base2, coef,
-            edge_a, edge_b,
-        ),
+        f32(tall, LANES),
+        [VMEM] * 9,
+        VMEM,
+        (pressure, storage, trans, source, base1, base2, coef, edge_a, edge_b),
     )
     side_c = lax.ppermute(side, "col", swaps(cols, False))
     side_d = lax.ppermute(side, "col", swaps(cols, True)) if cols > 2 else side_c

time: 50.5 us -> 49.7 us (0.984)
  Pallas kernels: 7.93 us -> 7.1 us
    pallas_call x7, Pallas kernels: 7.93 us -> 7.1 us  [call(): pl.pallas_call(kernel, out_shape=out_shape, in_specs=in_specs, out_specs=...]
  transfers between devices with their start and end apart: 16 -> 16, of which waited for: 7 -> 7; matrix products, arithmetic and copies ran while one was open for 0% -> 0% of each run, Pallas kernels for 13% -> 11%
where the time goes in v3:
time: 49.7 us; the launch traced here: 49.5 us
  starting transfers between devices  21.6 us (43%)
  waiting for transfers between devices  20.1 us (40%)
  Pallas kernels  7.1 us (14%)
  between operations  0.71 us (1%)
    ppermute x10, starting transfers between devices, chip_swap(): return lax.ppermute(value, 'slab', [(i, i ^ 2 * k) for i in range(slabs)])  17.1 us
    ppermute x10, waiting for transfers between devices, chip_swap(): return lax.ppermute(value, 'slab', [(i, i ^ 2 * k) for i in range(slabs)])  14 us
    pallas_call x7, Pallas kernels, call(): pl.pallas_call(kernel, out_shape=out_shape, in_specs=in_specs, out_specs=...  7.1 us
    ppermute x1, waiting for transfers between devices, shards(): side_c = lax.ppermute(side, 'col', swaps(cols, False))  2.48 us
    ppermute x1, waiting for transfers between devices, shards(): edge_b = lax.ppermute(edge_b, 'slab', shifts(slabs))  2.44 us
    ppermute x1, starting transfers between devices, shards(): edge_a = lax.ppermute(edge_a, 'slab', swaps(slabs, False))  2.21 us
    ppermute x1, starting transfers between devices, shards(): side_c = lax.ppermute(side, 'col', swaps(cols, False))  1.58 us
    ppermute x1, waiting for transfers between devices, shards(): other_rows = lax.ppermute(rows, 'slab', swaps(slabs, False))  1.24 us
  transfers between devices with their start and end apart: 16, of which 7 were waited for; matrix products, arithmetic and copies ran while one was open for 0% of the time, Pallas kernels for 11%

profile of v3, /device:TPU:0, one launch (start us, length us, event | category | flops | bytes accessed | tf_op | source)
XLA Modules:
  0.0 49.5 jit_solution(14499215793450011280)
XLA Ops:
  0.6 0.6 %collective-permute-start.4 = (f32[64,64,128]{2,1,0:T(8,128)}, f32[64,64,128]{2,1,0:T(8,128)S(1)}, u32[]{:S(2)}, u32[]{:S(2)}) collective-permute-start(f32[64,64,128]{2,1,0:T(8,128)} %bitcast.4), channel_id=1, source_target_pairs={{0,2},{2,0},{4,6},{6,4},{8,10},{10,8},{12,14},{14,12},{16,18},{18,... | collective-permute-start | bytes 6291464 | tf_op jit(solution)/shard_map/ppermute | solution.py:461
  1.2 2.5 %shard_map.104 = (f32[64,128]{1,0:T(8,128)S(1)}, f32[1,128]{1,0:T(1,128)S(1)}, s32[1,32]{1,0:T(1,128)S(1)}, s32[1,64]{1,0:T(1,128)S(1)}, s32[1,32]{1,0:T(1,128)S...) custom-call(f32[1,64]{1,0:T(1,128)} %bitcast.7, ...), custom_call_target="tpu_custom_call" | custom-call | tf_op jit(solution)/shard_map/pallas_call | solution.py:405
  3.7 0.1 collective-permute-start.1
  3.8 2.2 %collective-permute-start = (f32[7,8,256]{2,1,0:T(8,128)S(1)}, f32[7,8,256]{2,1,0:T(8,128)S(1)}, u32[]{:S(2)}, u32[]{:S(2)}) collective-permute-start(f32[7,8,256]{2,1,0:T(8,128)S(1)} %get-tuple-element.49), channel_id=1, source_target_pairs={{0,2},{2,0},{4,6},{6,4},{8,10},{10,8},{12,14},{14,12},{16,18},{18,... | collective-permute-start | bytes 172040 | tf_op jit(solution)/shard_map/ppermute | solution.py:492
  6.0 2.4 %collective-permute-done.1 = f32[7,8,256]{2,1,0:T(8,128)S(1)} collective-permute-done((f32[7,8,256]{2,1,0:T(8,128)S(1)}, f32[7,8,256]{2,1,0:T(8,128)S(1)}, u32[]{:S(2)}, u32[]{:S(2)}) %collective-permute-start.1) | collective-permute-done | bytes 57376 | tf_op jit(solution)/shard_map/ppermute | solution.py:490
  8.4 0.0 collective-permute-start.2
  8.4 0.0 collective-permute-done.4.other_ref
  8.4 0.2 shard_map.107
  8.6 3.7 %collective-permute-start.5 = (f32[4,64,128]{2,1,0:T(8,128)S(1)}, f32[4,64,128]{2,1,0:T(8,128)S(1)}, u32[]{:S(2)}, u32[]{:S(2)}) collective-permute-start(f32[4,64,128]{2,1,0:T(8,128)S(1)} %get-tuple-element.59), channel_id=1, source_target_pairs={{0,16},{2,18},{4,20},{6,22},{8,24},{10,26},{12,28},{14,30},{16,0},... | collective-permute-start | bytes 393224 | tf_op jit(solution)/shard_map/ppermute | solution.py:459
  12.3 1.6 %collective-permute-start.6 = (f32[4,64,128]{2,1,0:T(8,128)S(1)}, f32[4,64,128]{2,1,0:T(8,128)S(1)}, u32[]{:S(2)}, u32[]{:S(2)}) collective-permute-start(f32[4,64,128]{2,1,0:T(8,128)S(1)} %get-tuple-element.60), channel_id=1, source_target_pairs={{0,20},{2,22},{4,16},{6,18},{8,28},{10,30},{12,24},{14,26},{16,4},... | collective-permute-start | bytes 393224 | tf_op jit(solution)/shard_map/ppermute | solution.py:459
  14.0 0.0 collective-permute-done.refs_7_.a_ref
  14.0 0.0 collective-permute-done.2.refs_8_.b_ref
  14.0 0.2 shard_map.105
  14.2 1.6 %collective-permute-start.3 = (f32[80,128]{1,0:T(8,128)S(1)}, f32[80,128]{1,0:T(8,128)S(1)}, u32[]{:S(2)}, u32[]{:S(2)}) collective-permute-start(f32[80,128]{1,0:T(8,128)S(1)} %shard_map.105), channel_id=1, source_target_pairs={{0,1},{1,0},{2,3},{3,2},{4,5},{5,4},{6,7},{7,6},{8,9},{9,8},{10,11... | collective-permute-start | bytes 122888 | tf_op jit(solution)/shard_map/ppermute | solution.py:507
  15.8 2.5 %collective-permute-done.3.c_ref.d_ref = f32[80,128]{1,0:T(8,128)S(1)} collective-permute-done((f32[80,128]{1,0:T(8,128)S(1)}, f32[80,128]{1,0:T(8,128)S(1)}, u32[]{:S(2)}, u32[]{:S(2)}) %collective-permute-start.3) | collective-permute-done | bytes 40992 | tf_op jit(solution)/shard_map/ppermute | solution.py:507
  18.2 2.1 %shard_map.106 = (f32[64,256]{1,0:T(8,128)}, f32[16,8,128]{2,1,0:T(8,128)S(1)}) custom-call(s32[1,64]{1,0:T(1,128)S(1)} %get-tuple-element.40.place_ref, f32[1,128]{1,0:T(1,128)S(1)} %get-tuple-element.41.const_ref, f32[64,256]{1,0:T(8,128)S(1)} %get-tuple-element.42.refs_0_.p_ref, f32[64,256]{1,0:T(8,128)S(1)} %get-tuple-element.43.refs_1_.storage_ref, ...), custom_call_target="tpu_custom_call" | custom-call | tf_op jit(solution)/shard_map/pallas_call | solution.py:405
  20.3 0.1 collective-permute-start.8
  20.4 1.2 %collective-permute-done.8.other_ref = f32[16,8,128]{2,1,0:T(8,128)S(1)} collective-permute-done((f32[16,8,128]{2,1,0:T(8,128)S(1)}, f32[16,8,128]{2,1,0:T(8,128)S(1)}, u32[]{:S(2)}, u32[]{:S(2)}) %collective-permute-start.8) | collective-permute-done | bytes 65568 | tf_op jit(solution)/shard_map/ppermute | solution.py:528
  21.7 2.7 %collective-permute-start.13 = (f32[8,128]{1,0:T(8,128)S(1)}, f32[8,128]{1,0:T(8,128)S(1)}, u32[]{:S(2)}, u32[]{:S(2)}) collective-permute-start(f32[8,128]{1,0:T(8,128)S(1)} %get-tuple-element.75), channel_id=1, source_target_pairs={{0,16},{2,18},{4,20},{6,22},{8,24},{10,26},{12,28},{14,30},{16,0},... | collective-permute-start | bytes 12296 | tf_op jit(solution)/shard_map/ppermute | solution.py:459
  24.3 0.0 collective-permute-start.14
  24.3 1.8 %collective-permute-start.9 = (f32[4,72,128]{2,1,0:T(8,128)S(1)}, f32[4,72,128]{2,1,0:T(8,128)S(1)}, u32[]{:S(2)}, u32[]{:S(2)}) collective-permute-start(f32[4,72,128]{2,1,0:T(8,128)S(1)} %get-tuple-element.70), channel_id=1, source_target_pairs={{0,4},{2,6},{4,0},{6,2},{8,12},{10,14},{12,8},{14,10},{16,20},{18,... | collective-permute-start | bytes 442376 | tf_op jit(solution)/shard_map/ppermute | solution.py:459
  26.1 0.1 collective-permute-done.13.rest_5_
  26.3 1.6 %collective-permute-start.10 = (f32[4,72,128]{2,1,0:T(8,128)S(1)}, f32[4,72,128]{2,1,0:T(8,128)S(1)}, u32[]{:S(2)}, u32[]{:S(2)}) collective-permute-start(f32[4,72,128]{2,1,0:T(8,128)S(1)} %get-tuple-element.71), channel_id=1, source_target_pairs={{0,8},{2,10},{4,12},{6,14},{8,0},{10,2},{12,4},{14,6},{16,24},{18,... | collective-permute-start | bytes 442376 | tf_op jit(solution)/shard_map/ppermute | solution.py:459
  27.8 2.0 %collective-permute-done.14.rest_6_ = f32[8,128]{1,0:T(8,128)S(1)} collective-permute-done((f32[8,128]{1,0:T(8,128)S(1)}, f32[8,128]{1,0:T(8,128)S(1)}, u32[]{:S(2)}, u32[]{:S(2)}) %collective-permute-start.14) | collective-permute-done | bytes 4128 | tf_op jit(solution)/shard_map/ppermute | solution.py:459
  29.8 1.2 %collective-permute-start.11 = (f32[4,72,128]{2,1,0:T(8,128)S(1)}, f32[4,72,128]{2,1,0:T(8,128)S(1)}, u32[]{:S(2)}, u32[]{:S(2)}) collective-permute-start(f32[4,72,128]{2,1,0:T(8,128)S(1)} %get-tuple-element.72), channel_id=1, source_target_pairs={{0,12},{2,14},{4,8},{6,10},{8,4},{10,6},{12,0},{14,2},{16,28},{18,... | collective-permute-start | bytes 442376 | tf_op jit(solution)/shard_map/ppermute | solution.py:459
  31.0 0.0 collective-permute-done.5.rest_1_
  31.0 1.5 %collective-permute-start.12 = (f32[4,72,128]{2,1,0:T(8,128)S(1)}, f32[4,72,128]{2,1,0:T(8,128)S(1)}, u32[]{:S(2)}, u32[]{:S(2)}) collective-permute-start(f32[4,72,128]{2,1,0:T(8,128)S(1)} %get-tuple-element.73), channel_id=1, source_target_pairs={{0,28},{2,30},{4,24},{6,26},{8,20},{10,22},{12,16},{14,18},{16,12}... | collective-permute-start | bytes 442376 | tf_op jit(solution)/shard_map/ppermute | solution.py:459
  32.5 0.0 collective-permute-done.6.rest_2_
  32.6 1.6 %collective-permute-start.7 = (f32[4,64,128]{2,1,0:T(8,128)S(1)}, f32[4,64,128]{2,1,0:T(8,128)S(1)}, u32[]{:S(2)}, u32[]{:S(2)}) collective-permute-start(f32[4,64,128]{2,1,0:T(8,128)S(1)} %get-tuple-element.61), channel_id=1, source_target_pairs={{0,24},{2,26},{4,28},{6,30},{8,16},{10,18},{12,20},{14,22},{16,8},... | collective-permute-start | bytes 393224 | tf_op jit(solution)/shard_map/ppermute | solution.py:459
  34.1 8.4 %collective-permute-done.7.rest_3_ = f32[4,64,128]{2,1,0:T(8,128)S(1)} collective-permute-done((f32[4,64,128]{2,1,0:T(8,128)S(1)}, f32[4,64,128]{2,1,0:T(8,128)S(1)}, u32[]{:S(2)}, u32[]{:S(2)}) %collective-permute-start.7) | collective-permute-done | bytes 131104 | tf_op jit(solution)/shard_map/ppermute | solution.py:459
  42.5 1.4 %collective-permute-start.15 = (f32[8,128]{1,0:T(8,128)S(1)}, f32[8,128]{1,0:T(8,128)S(1)}, u32[]{:S(2)}, u32[]{:S(2)}) collective-permute-start(f32[8,128]{1,0:T(8,128)S(1)} %get-tuple-element.77), channel_id=1, source_target_pairs={{0,24},{2,26},{4,28},{6,30},{8,16},{10,18},{12,20},{14,22},{16,8},... | collective-permute-start | bytes 12296 | tf_op jit(solution)/shard_map/ppermute | solution.py:459
  43.9 0.5 %shard_map.108 = (bf16[64,192]{1,0:T(8,128)(2,1)S(1)}, f32[2,64,128]{2,1,0:T(8,128)S(1)}, f32[16,64,128]{2,1,0:T(8,128)S(1)}) custom-call(f32[1,64]{1,0:T(1,128)S(1)} %get-tuple-element.53.cap_ref, f32[1,64]{1,0:T(1,128)S(1)} %get-tuple-element.54.trans_ref, f32[64,128]{1,0:T(8,128)S(1)} %get-tuple-element.55.inv_ref, ...), custom_call_target="tpu_custom_call" | custom-call | tf_op jit(solution)/shard_map/pallas_call | solution.py:405
  44.4 3.5 %collective-permute-done.15.rest_7_ = f32[8,128]{1,0:T(8,128)S(1)} collective-permute-done((f32[8,128]{1,0:T(8,128)S(1)}, f32[8,128]{1,0:T(8,128)S(1)}, u32[]{:S(2)}, u32[]{:S(2)}) %collective-permute-start.15) | collective-permute-done | bytes 4128 | tf_op jit(solution)/shard_map/ppermute | solution.py:459
  47.9 0.0 collective-permute-done.9.rest_0_
  47.9 0.0 collective-permute-done.10.rest_1_
  47.9 0.0 collective-permute-done.11.rest_2_
  47.9 0.0 collective-permute-done.12.rest_3_
  47.9 1.6 %shard_map.110 = f32[32,64,128]{2,1,0:T(8,128)} custom-call(s32[1,32]{1,0:T(1,128)S(1)} %get-tuple-element.52.recv_ref, bf16[64,192]{1,0:T(8,128)(2,1)S(1)} %get-tuple-element.62.left_ref, f32[2,64,128]{2,1,0:T(8,128)S(1)} %get-tuple-element.63.m_ref, f32[16,64,128]{2,1,0:T(8,128)S(1)} %get-tuple-element.64.product_ref, ...), custom_call_target="tpu_custom_call" | custom-call | tf_op jit(solution)/shard_map/pallas_call | solution.py:405
  (1 shorter events, 0.0 us)
Async XLA Ops:
  0.6 7.8 %collective-permute-start.4 = (f32[64,64,128]{2,1,0:T(8,128)}, f32[64,64,128]{2,1,0:T(8,128)S(1)}, u32[]{:S(2)}, u32[]{:S(2)}) collective-permute-start(f32[64,64,128]{2,1,0:T(8,128)} %bitcast.4), channel_id=1, source_target_pairs={{0,2},{2,0},{4,6},{6,4},{8,10},{10,8},{12,14},{14,12},{16,18},{18,... | collective-permute-start | bytes 6291464 | tf_op jit(solution)/shard_map/ppermute | solution.py:461
  3.7 4.7 %collective-permute-start.1 = (f32[7,8,256]{2,1,0:T(8,128)S(1)}, f32[7,8,256]{2,1,0:T(8,128)S(1)}, u32[]{:S(2)}, u32[]{:S(2)}) collective-permute-start(f32[7,8,256]{2,1,0:T(8,128)S(1)} %get-tuple-element.50), channel_id=1, source_target_pairs={{0,2},{2,6},{4,0},{6,10},{8,4},{10,14},{12,8},{14,18},{16,12},{18,... | collective-permute-start | bytes 172040 | tf_op jit(solution)/shard_map/ppermute | solution.py:490
  3.8 10.2 %collective-permute-start = (f32[7,8,256]{2,1,0:T(8,128)S(1)}, f32[7,8,256]{2,1,0:T(8,128)S(1)}, u32[]{:S(2)}, u32[]{:S(2)}) collective-permute-start(f32[7,8,256]{2,1,0:T(8,128)S(1)} %get-tuple-element.49), channel_id=1, source_target_pairs={{0,2},{2,0},{4,6},{6,4},{8,10},{10,8},{12,14},{14,12},{16,18},{18,... | collective-permute-start | bytes 172040 | tf_op jit(solution)/shard_map/ppermute | solution.py:492
  8.4 5.5 %collective-permute-start.2 = (f32[7,8,256]{2,1,0:T(8,128)S(1)}, f32[7,8,256]{2,1,0:T(8,128)S(1)}, u32[]{:S(2)}, u32[]{:S(2)}) collective-permute-start(f32[7,8,256]{2,1,0:T(8,128)S(1)} %collective-permute-done.1), channel_id=1, source_target_pairs={{0,2},{2,0},{4,6},{6,4},{8,10},{10,8},{12,14},{14,12},{16,18},{18,... | collective-permute-start | bytes 172040 | tf_op jit(solution)/shard_map/ppermute | solution.py:491
  8.6 22.4 %collective-permute-start.5 = (f32[4,64,128]{2,1,0:T(8,128)S(1)}, f32[4,64,128]{2,1,0:T(8,128)S(1)}, u32[]{:S(2)}, u32[]{:S(2)}) collective-permute-start(f32[4,64,128]{2,1,0:T(8,128)S(1)} %get-tuple-element.59), channel_id=1, source_target_pairs={{0,16},{2,18},{4,20},{6,22},{8,24},{10,26},{12,28},{14,30},{16,0},... | collective-permute-start | bytes 393224 | tf_op jit(solution)/shard_map/ppermute | solution.py:459
  12.3 20.2 %collective-permute-start.6 = (f32[4,64,128]{2,1,0:T(8,128)S(1)}, f32[4,64,128]{2,1,0:T(8,128)S(1)}, u32[]{:S(2)}, u32[]{:S(2)}) collective-permute-start(f32[4,64,128]{2,1,0:T(8,128)S(1)} %get-tuple-element.60), channel_id=1, source_target_pairs={{0,20},{2,22},{4,16},{6,18},{8,28},{10,30},{12,24},{14,26},{16,4},... | collective-permute-start | bytes 393224 | tf_op jit(solution)/shard_map/ppermute | solution.py:459
  14.2 4.1 %collective-permute-start.3 = (f32[80,128]{1,0:T(8,128)S(1)}, f32[80,128]{1,0:T(8,128)S(1)}, u32[]{:S(2)}, u32[]{:S(2)}) collective-permute-start(f32[80,128]{1,0:T(8,128)S(1)} %shard_map.105), channel_id=1, source_target_pairs={{0,1},{1,0},{2,3},{3,2},{4,5},{5,4},{6,7},{7,6},{8,9},{9,8},{10,11... | collective-permute-start | bytes 122888 | tf_op jit(solution)/shard_map/ppermute | solution.py:507
  20.3 1.3 %collective-permute-start.8 = (f32[16,8,128]{2,1,0:T(8,128)S(1)}, f32[16,8,128]{2,1,0:T(8,128)S(1)}, u32[]{:S(2)}, u32[]{:S(2)}) collective-permute-start(f32[16,8,128]{2,1,0:T(8,128)S(1)} %get-tuple-element.65.own_ref), channel_id=1, source_target_pairs={{0,2},{2,0},{4,6},{6,4},{8,10},{10,8},{12,14},{14,12},{16,18},{18,... | collective-permute-start | bytes 196616 | tf_op jit(solution)/shard_map/ppermute | solution.py:528
  21.7 4.6 %collective-permute-start.13 = (f32[8,128]{1,0:T(8,128)S(1)}, f32[8,128]{1,0:T(8,128)S(1)}, u32[]{:S(2)}, u32[]{:S(2)}) collective-permute-start(f32[8,128]{1,0:T(8,128)S(1)} %get-tuple-element.75), channel_id=1, source_target_pairs={{0,16},{2,18},{4,20},{6,22},{8,24},{10,26},{12,28},{14,30},{16,0},... | collective-permute-start | bytes 12296 | tf_op jit(solution)/shard_map/ppermute | solution.py:459
  24.3 5.5 %collective-permute-start.14 = (f32[8,128]{1,0:T(8,128)S(1)}, f32[8,128]{1,0:T(8,128)S(1)}, u32[]{:S(2)}, u32[]{:S(2)}) collective-permute-start(f32[8,128]{1,0:T(8,128)S(1)} %get-tuple-element.76), channel_id=1, source_target_pairs={{0,20},{2,22},{4,16},{6,18},{8,28},{10,30},{12,24},{14,26},{16,4},... | collective-permute-start | bytes 12296 | tf_op jit(solution)/shard_map/ppermute | solution.py:459
  24.3 23.5 %collective-permute-start.9 = (f32[4,72,128]{2,1,0:T(8,128)S(1)}, f32[4,72,128]{2,1,0:T(8,128)S(1)}, u32[]{:S(2)}, u32[]{:S(2)}) collective-permute-start(f32[4,72,128]{2,1,0:T(8,128)S(1)} %get-tuple-element.70), channel_id=1, source_target_pairs={{0,4},{2,6},{4,0},{6,2},{8,12},{10,14},{12,8},{14,10},{16,20},{18,... | collective-permute-start | bytes 442376 | tf_op jit(solution)/shard_map/ppermute | solution.py:459
  26.3 21.6 %collective-permute-start.10 = (f32[4,72,128]{2,1,0:T(8,128)S(1)}, f32[4,72,128]{2,1,0:T(8,128)S(1)}, u32[]{:S(2)}, u32[]{:S(2)}) collective-permute-start(f32[4,72,128]{2,1,0:T(8,128)S(1)} %get-tuple-element.71), channel_id=1, source_target_pairs={{0,8},{2,10},{4,12},{6,14},{8,0},{10,2},{12,4},{14,6},{16,24},{18,... | collective-permute-start | bytes 442376 | tf_op jit(solution)/shard_map/ppermute | solution.py:459
  29.8 18.0 %collective-permute-start.11 = (f32[4,72,128]{2,1,0:T(8,128)S(1)}, f32[4,72,128]{2,1,0:T(8,128)S(1)}, u32[]{:S(2)}, u32[]{:S(2)}) collective-permute-start(f32[4,72,128]{2,1,0:T(8,128)S(1)} %get-tuple-element.72), channel_id=1, source_target_pairs={{0,12},{2,14},{4,8},{6,10},{8,4},{10,6},{12,0},{14,2},{16,28},{18,... | collective-permute-start | bytes 442376 | tf_op jit(solution)/shard_map/ppermute | solution.py:459
  31.0 16.8 %collective-permute-start.12 = (f32[4,72,128]{2,1,0:T(8,128)S(1)}, f32[4,72,128]{2,1,0:T(8,128)S(1)}, u32[]{:S(2)}, u32[]{:S(2)}) collective-permute-start(f32[4,72,128]{2,1,0:T(8,128)S(1)} %get-tuple-element.73), channel_id=1, source_target_pairs={{0,28},{2,30},{4,24},{6,26},{8,20},{10,22},{12,16},{14,18},{16,12}... | collective-permute-start | bytes 442376 | tf_op jit(solution)/shard_map/ppermute | solution.py:459
  32.6 9.9 %collective-permute-start.7 = (f32[4,64,128]{2,1,0:T(8,128)S(1)}, f32[4,64,128]{2,1,0:T(8,128)S(1)}, u32[]{:S(2)}, u32[]{:S(2)}) collective-permute-start(f32[4,64,128]{2,1,0:T(8,128)S(1)} %get-tuple-element.61), channel_id=1, source_target_pairs={{0,24},{2,26},{4,28},{6,30},{8,16},{10,18},{12,20},{14,22},{16,8},... | collective-permute-start | bytes 393224 | tf_op jit(solution)/shard_map/ppermute | solution.py:459
  42.5 5.4 %collective-permute-start.15 = (f32[8,128]{1,0:T(8,128)S(1)}, f32[8,128]{1,0:T(8,128)S(1)}, u32[]{:S(2)}, u32[]{:S(2)}) collective-permute-start(f32[8,128]{1,0:T(8,128)S(1)} %get-tuple-element.77), channel_id=1, source_target_pairs={{0,24},{2,26},{4,28},{6,30},{8,16},{10,18},{12,20},{14,22},{16,8},... | collective-permute-start | bytes 12296 | tf_op jit(solution)/shard_map/ppermute | solution.py:459

commit v4 on v3

--- a/solution.py
+++ b/solution.py
@@ -137,7 +137,7 @@
         for i in range(chunks):
             chunk(i).start()
 
-    for load in loads:
+    for load in loads[:2]:
         load.wait()
     cap_row, trans_row = cap_ref[...], trans_ref[...]
     inverse, cap = inverse_of(cap_row, trans_row)
@@ -152,6 +152,8 @@
     coupling = t0 * (1.0 - c0)
     const_ref[...] = jnp.broadcast_to(t0 * c1 / coupling, const_ref.shape)
 
+    for load in loads[2:]:
+        load.wait()
     tiles[...] = jnp.zeros_like(tiles)
 
     @pl.when(even)
@@ -208,7 +210,7 @@
     def fill(source):
         for k, ref in enumerate(out_refs):
             for r in range(CAP):
-                ref[r, :count] = source[slot_ref[0, k * CAP + r]]
+                ref[r * count : (r + 1) * count] = source[slot_ref[0, k * CAP + r]]
 
     @pl.when(core == 0)
     def _():
@@ -230,7 +232,7 @@
     local_ref[...] = rows(0)
     for k, ref in zip(late_k, outs):
         value = rows(k)
-        ref[0, ref.shape[1] - value.shape[0] :] = value
+        ref[ref.shape[0] - value.shape[0] :] = value
     for k, ref in zip(early_k, outs[len(late_k) :]):
         ref[...] = rows(k)
 
@@ -346,6 +348,10 @@
     return results
 
 
+def parts_of(ref, count):
+    return [ref[r * count : (r + 1) * count] for r in range(CAP)]
+
+
 def product_kernel(cap_ref, trans_ref, inv_ref, *rest):
     *blocks, left_ref, m_ref, out_ref = rest
     count = cap_ref.shape[1]
@@ -362,7 +368,7 @@
     m_ref[0] = jnp.broadcast_to(couple2, (count, LANES))
     m_ref[1] = jnp.broadcast_to(couple, (count, LANES))
     for i, ref in enumerate(blocks):
-        for r, value in enumerate(multiply(left, [ref[r, :count] for r in range(CAP)])):
+        for r, value in enumerate(multiply(left, parts_of(ref, count))):
             out_ref[i * CAP + r] = value
 
 
@@ -375,9 +381,9 @@
         held[pl.ds(k * CAP, CAP)] = product_ref[pl.ds(i * CAP, CAP)]
     left = left_ref[...]
     for k, ref in zip(tailed_k, in_refs):
-        rows[k] = ref[0, count:]
+        rows[k] = ref[CAP * count :]
         if k not in ready_k:
-            for r, value in enumerate(multiply(left, [ref[r, :count] for r in range(CAP)])):
+            for r, value in enumerate(multiply(left, parts_of(ref, count))):
                 held[k * CAP + r] = value
     for k, ref in zip(loose_k, in_refs[len(tailed_k) :]):
         rows[k] = ref[...]
@@ -492,7 +498,7 @@
     edge_a = lax.ppermute(edge_a, "slab", swaps(slabs, False))
     packed = call(
         pack_kernel,
-        tuple(f32(CAP, count + (tail if k in late_k else 0), cells) for k in range(chips)),
+        tuple(f32(CAP * count + (tail if k in late_k else 0), cells) for k in range(chips)),
         [VMEM, VMEM, VMEM],
         (VMEM,) * chips,
         (slot, held, hopped),
@@ -529,7 +535,7 @@
     local_rows, *filled = call(
         functools.partial(rows_kernel, late_k, early_k),
         (f32(tail, cells),)
-        + (f32(CAP, count + tail, cells),) * len(late_k)
+        + (f32(CAP * count + tail, cells),) * len(late_k)
         + (f32(tail, cells),) * len(early_k),
         [VMEM] * (2 + len(late_k)),
         (VMEM,) * chips,

time: 49.7 us -> 43 us (0.87)
  waiting for transfers between devices: 20.1 us -> 12.7 us
  starting transfers between devices: 21.6 us -> 22.3 us
    ppermute x10, waiting for transfers between devices: 14 us -> 6.34 us  [chip_swap(): return lax.ppermute(value, 'slab', [(i, i ^ 2 * k) for i in range(slabs)])]
    ppermute x10, starting transfers between devices: 17.1 us -> 18.1 us  [chip_swap(): return lax.ppermute(value, 'slab', [(i, i ^ 2 * k) for i in range(slabs)])]
  transfers between devices with their start and end apart: 16 -> 16, of which waited for: 7 -> 5; matrix products, arithmetic and copies ran while one was open for 0% -> 0% of each run, Pallas kernels for 11% -> 13%
where the time goes in v4:
time: 43 us; the launch traced here: 42.8 us
  starting transfers between devices  22.3 us (52%)
  waiting for transfers between devices  12.7 us (30%)
  Pallas kernels  7.04 us (16%)
  between operations  0.72 us (2%)
    ppermute x10, starting transfers between devices, chip_swap(): return lax.ppermute(value, 'slab', [(i, i ^ 2 * k) for i in range(slabs)])  18.1 us
    pallas_call x7, Pallas kernels, call(): pl.pallas_call(kernel, out_shape=out_shape, in_specs=in_specs, out_specs=...  7.04 us
    ppermute x10, waiting for transfers between devices, chip_swap(): return lax.ppermute(value, 'slab', [(i, i ^ 2 * k) for i in range(slabs)])  6.34 us
    ppermute x1, waiting for transfers between devices, shards(): edge_b = lax.ppermute(edge_b, 'slab', shifts(slabs))  2.66 us
    ppermute x1, waiting for transfers between devices, shards(): side_c = lax.ppermute(side, 'col', swaps(cols, False))  2.48 us
    ppermute x1, starting transfers between devices, shards(): edge_a = lax.ppermute(edge_a, 'slab', swaps(slabs, False))  1.99 us
    ppermute x1, starting transfers between devices, shards(): side_c = lax.ppermute(side, 'col', swaps(cols, False))  1.58 us
    ppermute x1, waiting for transfers between devices, shards(): other_rows = lax.ppermute(rows, 'slab', swaps(slabs, False))  1.24 us
  transfers between devices with their start and end apart: 16, of which 5 were waited for; matrix products, arithmetic and copies ran while one was open for 0% of the time, Pallas kernels for 13%

profile of v4, /device:TPU:0, one launch (start us, length us, event | category | flops | bytes accessed | tf_op | source)
XLA Modules:
  0.0 42.8 jit_solution(263918364327578993)
XLA Ops:
  0.6 0.6 %collective-permute-start.4 = (f32[64,64,128]{2,1,0:T(8,128)}, f32[64,64,128]{2,1,0:T(8,128)S(1)}, u32[]{:S(2)}, u32[]{:S(2)}) collective-permute-start(f32[64,64,128]{2,1,0:T(8,128)} %bitcast.4), channel_id=1, source_target_pairs={{0,2},{2,0},{4,6},{6,4},{8,10},{10,8},{12,14},{14,12},{16,18},{18,... | collective-permute-start | bytes 6291464 | tf_op jit(solution)/shard_map/ppermute | solution.py:467
  1.2 2.5 %shard_map.104 = (f32[64,128]{1,0:T(8,128)S(1)}, f32[1,128]{1,0:T(1,128)S(1)}, s32[1,32]{1,0:T(1,128)S(1)}, s32[1,64]{1,0:T(1,128)S(1)}, s32[1,32]{1,0:T(1,128)S...) custom-call(f32[1,64]{1,0:T(1,128)} %bitcast.7, ...), custom_call_target="tpu_custom_call" | custom-call | tf_op jit(solution)/shard_map/pallas_call | solution.py:411
  3.7 0.1 collective-permute-start.1
  3.7 2.0 %collective-permute-start = (f32[7,8,256]{2,1,0:T(8,128)S(1)}, f32[7,8,256]{2,1,0:T(8,128)S(1)}, u32[]{:S(2)}, u32[]{:S(2)}) collective-permute-start(f32[7,8,256]{2,1,0:T(8,128)S(1)} %get-tuple-element.49), channel_id=1, source_target_pairs={{0,2},{2,0},{4,6},{6,4},{8,10},{10,8},{12,14},{14,12},{16,18},{18,... | collective-permute-start | bytes 172040 | tf_op jit(solution)/shard_map/ppermute | solution.py:498
  5.7 2.7 %collective-permute-done.1 = f32[7,8,256]{2,1,0:T(8,128)S(1)} collective-permute-done((f32[7,8,256]{2,1,0:T(8,128)S(1)}, f32[7,8,256]{2,1,0:T(8,128)S(1)}, u32[]{:S(2)}, u32[]{:S(2)}) %collective-permute-start.1) | collective-permute-done | bytes 57376 | tf_op jit(solution)/shard_map/ppermute | solution.py:496
  8.4 0.0 collective-permute-start.2
  8.4 0.0 collective-permute-done.4.other_ref
  8.4 0.2 shard_map.107
  8.6 3.5 %collective-permute-start.5 = (f32[256,128]{1,0:T(8,128)S(1)}, f32[256,128]{1,0:T(8,128)S(1)}, u32[]{:S(2)}, u32[]{:S(2)}) collective-permute-start(f32[256,128]{1,0:T(8,128)S(1)} %get-tuple-element.59), channel_id=1, source_target_pairs={{0,16},{2,18},{4,20},{6,22},{8,24},{10,26},{12,28},{14,30},{16,0},... | collective-permute-start | bytes 393224 | tf_op jit(solution)/shard_map/ppermute | solution.py:465
  12.1 1.8 %collective-permute-start.6 = (f32[256,128]{1,0:T(8,128)S(1)}, f32[256,128]{1,0:T(8,128)S(1)}, u32[]{:S(2)}, u32[]{:S(2)}) collective-permute-start(f32[256,128]{1,0:T(8,128)S(1)} %get-tuple-element.60), channel_id=1, source_target_pairs={{0,20},{2,22},{4,16},{6,18},{8,28},{10,30},{12,24},{14,26},{16,4},... | collective-permute-start | bytes 393224 | tf_op jit(solution)/shard_map/ppermute | solution.py:465
  13.9 0.0 collective-permute-done.refs_7_.a_ref
  13.9 0.0 collective-permute-done.2.refs_8_.b_ref
  13.9 0.2 shard_map.105
  14.1 1.6 %collective-permute-start.3 = (f32[80,128]{1,0:T(8,128)S(1)}, f32[80,128]{1,0:T(8,128)S(1)}, u32[]{:S(2)}, u32[]{:S(2)}) collective-permute-start(f32[80,128]{1,0:T(8,128)S(1)} %shard_map.105), channel_id=1, source_target_pairs={{0,1},{1,0},{2,3},{3,2},{4,5},{5,4},{6,7},{7,6},{8,9},{9,8},{10,11... | collective-permute-start | bytes 122888 | tf_op jit(solution)/shard_map/ppermute | solution.py:513
  15.7 2.5 %collective-permute-done.3.c_ref.d_ref = f32[80,128]{1,0:T(8,128)S(1)} collective-permute-done((f32[80,128]{1,0:T(8,128)S(1)}, f32[80,128]{1,0:T(8,128)S(1)}, u32[]{:S(2)}, u32[]{:S(2)}) %collective-permute-start.3) | collective-permute-done | bytes 40992 | tf_op jit(solution)/shard_map/ppermute | solution.py:513
  18.2 2.1 %shard_map.106 = (f32[64,256]{1,0:T(8,128)}, f32[16,8,128]{2,1,0:T(8,128)S(1)}) custom-call(s32[1,64]{1,0:T(1,128)S(1)} %get-tuple-element.40.place_ref, f32[1,128]{1,0:T(1,128)S(1)} %get-tuple-element.41.const_ref, f32[64,256]{1,0:T(8,128)S(1)} %get-tuple-element.42.refs_0_.p_ref, f32[64,256]{1,0:T(8,128)S(1)} %get-tuple-element.43.refs_1_.storage_ref, ...), custom_call_target="tpu_custom_call" | custom-call | tf_op jit(solution)/shard_map/pallas_call | solution.py:411
  20.3 0.1 collective-permute-start.8
  20.4 1.2 %collective-permute-done.8.other_ref = f32[16,8,128]{2,1,0:T(8,128)S(1)} collective-permute-done((f32[16,8,128]{2,1,0:T(8,128)S(1)}, f32[16,8,128]{2,1,0:T(8,128)S(1)}, u32[]{:S(2)}, u32[]{:S(2)}) %collective-permute-start.8) | collective-permute-done | bytes 65568 | tf_op jit(solution)/shard_map/ppermute | solution.py:534
  21.6 2.7 %collective-permute-start.13 = (f32[8,128]{1,0:T(8,128)S(1)}, f32[8,128]{1,0:T(8,128)S(1)}, u32[]{:S(2)}, u32[]{:S(2)}) collective-permute-start(f32[8,128]{1,0:T(8,128)S(1)} %get-tuple-element.75), channel_id=1, source_target_pairs={{0,16},{2,18},{4,20},{6,22},{8,24},{10,26},{12,28},{14,30},{16,0},... | collective-permute-start | bytes 12296 | tf_op jit(solution)/shard_map/ppermute | solution.py:465
  24.3 0.0 collective-permute-start.14
  24.3 3.3 %collective-permute-start.7 = (f32[256,128]{1,0:T(8,128)S(1)}, f32[256,128]{1,0:T(8,128)S(1)}, u32[]{:S(2)}, u32[]{:S(2)}) collective-permute-start(f32[256,128]{1,0:T(8,128)S(1)} %get-tuple-element.61), channel_id=1, source_target_pairs={{0,24},{2,26},{4,28},{6,30},{8,16},{10,18},{12,20},{14,22},{16,8},... | collective-permute-start | bytes 393224 | tf_op jit(solution)/shard_map/ppermute | solution.py:465
  27.6 0.0 collective-permute-done.13.rest_5_
  27.6 0.0 collective-permute-start.9
  27.6 3.8 %collective-permute-done.14.rest_6_ = f32[8,128]{1,0:T(8,128)S(1)} collective-permute-done((f32[8,128]{1,0:T(8,128)S(1)}, f32[8,128]{1,0:T(8,128)S(1)}, u32[]{:S(2)}, u32[]{:S(2)}) %collective-permute-start.14) | collective-permute-done | bytes 4128 | tf_op jit(solution)/shard_map/ppermute | solution.py:465
  31.4 0.0 collective-permute-start.10
  31.4 0.0 collective-permute-done.5.rest_1_
  31.4 0.0 collective-permute-start.11
  31.4 0.0 collective-permute-done.6.rest_2_
  31.4 3.2 %collective-permute-start.12 = (f32[264,128]{1,0:T(8,128)S(1)}, f32[264,128]{1,0:T(8,128)S(1)}, u32[]{:S(2)}, u32[]{:S(2)}) collective-permute-start(f32[264,128]{1,0:T(8,128)S(1)} %get-tuple-element.73), channel_id=1, source_target_pairs={{0,28},{2,30},{4,24},{6,26},{8,20},{10,22},{12,16},{14,18},{16,12}... | collective-permute-start | bytes 405512 | tf_op jit(solution)/shard_map/ppermute | solution.py:465
  34.7 0.0 collective-permute-done.7.rest_3_
  34.7 3.5 %collective-permute-start.15 = (f32[8,128]{1,0:T(8,128)S(1)}, f32[8,128]{1,0:T(8,128)S(1)}, u32[]{:S(2)}, u32[]{:S(2)}) collective-permute-start(f32[8,128]{1,0:T(8,128)S(1)} %get-tuple-element.77), channel_id=1, source_target_pairs={{0,24},{2,26},{4,28},{6,30},{8,16},{10,18},{12,20},{14,22},{16,8},... | collective-permute-start | bytes 12296 | tf_op jit(solution)/shard_map/ppermute | solution.py:465
  38.1 0.5 %shard_map.108 = (bf16[64,192]{1,0:T(8,128)(2,1)S(1)}, f32[2,64,128]{2,1,0:T(8,128)S(1)}, f32[16,64,128]{2,1,0:T(8,128)S(1)}) custom-call(f32[1,64]{1,0:T(1,128)S(1)} %get-tuple-element.53.cap_ref, f32[1,64]{1,0:T(1,128)S(1)} %get-tuple-element.54.trans_ref, f32[64,128]{1,0:T(8,128)S(1)} %get-tuple-element.55.inv_ref, ...), custom_call_target="tpu_custom_call" | custom-call | tf_op jit(solution)/shard_map/pallas_call | solution.py:411
  38.6 2.5 %collective-permute-done.15.rest_7_ = f32[8,128]{1,0:T(8,128)S(1)} collective-permute-done((f32[8,128]{1,0:T(8,128)S(1)}, f32[8,128]{1,0:T(8,128)S(1)}, u32[]{:S(2)}, u32[]{:S(2)}) %collective-permute-start.15) | collective-permute-done | bytes 4128 | tf_op jit(solution)/shard_map/ppermute | solution.py:465
  41.2 0.0 collective-permute-done.9.rest_0_
  41.2 0.0 collective-permute-done.10.rest_1_
  41.2 0.0 collective-permute-done.11.rest_2_
  41.2 0.0 collective-permute-done.12.rest_3_
  41.2 1.6 %shard_map.110 = f32[32,64,128]{2,1,0:T(8,128)} custom-call(s32[1,32]{1,0:T(1,128)S(1)} %get-tuple-element.52.recv_ref, bf16[64,192]{1,0:T(8,128)(2,1)S(1)} %get-tuple-element.62.left_ref, f32[2,64,128]{2,1,0:T(8,128)S(1)} %get-tuple-element.63.m_ref, f32[16,64,128]{2,1,0:T(8,128)S(1)} %get-tuple-element.64.product_ref, ...), custom_call_target="tpu_custom_call" | custom-call | tf_op jit(solution)/shard_map/pallas_call | solution.py:411
  (1 shorter events, 0.0 us)
Async XLA Ops:
  0.6 7.7 %collective-permute-start.4 = (f32[64,64,128]{2,1,0:T(8,128)}, f32[64,64,128]{2,1,0:T(8,128)S(1)}, u32[]{:S(2)}, u32[]{:S(2)}) collective-permute-start(f32[64,64,128]{2,1,0:T(8,128)} %bitcast.4), channel_id=1, source_target_pairs={{0,2},{2,0},{4,6},{6,4},{8,10},{10,8},{12,14},{14,12},{16,18},{18,... | collective-permute-start | bytes 6291464 | tf_op jit(solution)/shard_map/ppermute | solution.py:467
  3.7 4.7 %collective-permute-start.1 = (f32[7,8,256]{2,1,0:T(8,128)S(1)}, f32[7,8,256]{2,1,0:T(8,128)S(1)}, u32[]{:S(2)}, u32[]{:S(2)}) collective-permute-start(f32[7,8,256]{2,1,0:T(8,128)S(1)} %get-tuple-element.50), channel_id=1, source_target_pairs={{0,2},{2,6},{4,0},{6,10},{8,4},{10,14},{12,8},{14,18},{16,12},{18,... | collective-permute-start | bytes 172040 | tf_op jit(solution)/shard_map/ppermute | solution.py:496
  3.7 10.2 %collective-permute-start = (f32[7,8,256]{2,1,0:T(8,128)S(1)}, f32[7,8,256]{2,1,0:T(8,128)S(1)}, u32[]{:S(2)}, u32[]{:S(2)}) collective-permute-start(f32[7,8,256]{2,1,0:T(8,128)S(1)} %get-tuple-element.49), channel_id=1, source_target_pairs={{0,2},{2,0},{4,6},{6,4},{8,10},{10,8},{12,14},{14,12},{16,18},{18,... | collective-permute-start | bytes 172040 | tf_op jit(solution)/shard_map/ppermute | solution.py:498
  8.4 5.5 %collective-permute-start.2 = (f32[7,8,256]{2,1,0:T(8,128)S(1)}, f32[7,8,256]{2,1,0:T(8,128)S(1)}, u32[]{:S(2)}, u32[]{:S(2)}) collective-permute-start(f32[7,8,256]{2,1,0:T(8,128)S(1)} %collective-permute-done.1), channel_id=1, source_target_pairs={{0,2},{2,0},{4,6},{6,4},{8,10},{10,8},{12,14},{14,12},{16,18},{18,... | collective-permute-start | bytes 172040 | tf_op jit(solution)/shard_map/ppermute | solution.py:497
  8.6 22.8 %collective-permute-start.5 = (f32[256,128]{1,0:T(8,128)S(1)}, f32[256,128]{1,0:T(8,128)S(1)}, u32[]{:S(2)}, u32[]{:S(2)}) collective-permute-start(f32[256,128]{1,0:T(8,128)S(1)} %get-tuple-element.59), channel_id=1, source_target_pairs={{0,16},{2,18},{4,20},{6,22},{8,24},{10,26},{12,28},{14,30},{16,0},... | collective-permute-start | bytes 393224 | tf_op jit(solution)/shard_map/ppermute | solution.py:465
  12.1 19.3 %collective-permute-start.6 = (f32[256,128]{1,0:T(8,128)S(1)}, f32[256,128]{1,0:T(8,128)S(1)}, u32[]{:S(2)}, u32[]{:S(2)}) collective-permute-start(f32[256,128]{1,0:T(8,128)S(1)} %get-tuple-element.60), channel_id=1, source_target_pairs={{0,20},{2,22},{4,16},{6,18},{8,28},{10,30},{12,24},{14,26},{16,4},... | collective-permute-start | bytes 393224 | tf_op jit(solution)/shard_map/ppermute | solution.py:465
  14.1 4.1 %collective-permute-start.3 = (f32[80,128]{1,0:T(8,128)S(1)}, f32[80,128]{1,0:T(8,128)S(1)}, u32[]{:S(2)}, u32[]{:S(2)}) collective-permute-start(f32[80,128]{1,0:T(8,128)S(1)} %shard_map.105), channel_id=1, source_target_pairs={{0,1},{1,0},{2,3},{3,2},{4,5},{5,4},{6,7},{7,6},{8,9},{9,8},{10,11... | collective-permute-start | bytes 122888 | tf_op jit(solution)/shard_map/ppermute | solution.py:513
  20.3 1.3 %collective-permute-start.8 = (f32[16,8,128]{2,1,0:T(8,128)S(1)}, f32[16,8,128]{2,1,0:T(8,128)S(1)}, u32[]{:S(2)}, u32[]{:S(2)}) collective-permute-start(f32[16,8,128]{2,1,0:T(8,128)S(1)} %get-tuple-element.65.own_ref), channel_id=1, source_target_pairs={{0,2},{2,0},{4,6},{6,4},{8,10},{10,8},{12,14},{14,12},{16,18},{18,... | collective-permute-start | bytes 196616 | tf_op jit(solution)/shard_map/ppermute | solution.py:534
  21.6 6.0 %collective-permute-start.13 = (f32[8,128]{1,0:T(8,128)S(1)}, f32[8,128]{1,0:T(8,128)S(1)}, u32[]{:S(2)}, u32[]{:S(2)}) collective-permute-start(f32[8,128]{1,0:T(8,128)S(1)} %get-tuple-element.75), channel_id=1, source_target_pairs={{0,16},{2,18},{4,20},{6,22},{8,24},{10,26},{12,28},{14,30},{16,0},... | collective-permute-start | bytes 12296 | tf_op jit(solution)/shard_map/ppermute | solution.py:465
  24.3 7.1 %collective-permute-start.14 = (f32[8,128]{1,0:T(8,128)S(1)}, f32[8,128]{1,0:T(8,128)S(1)}, u32[]{:S(2)}, u32[]{:S(2)}) collective-permute-start(f32[8,128]{1,0:T(8,128)S(1)} %get-tuple-element.76), channel_id=1, source_target_pairs={{0,20},{2,22},{4,16},{6,18},{8,28},{10,30},{12,24},{14,26},{16,4},... | collective-permute-start | bytes 12296 | tf_op jit(solution)/shard_map/ppermute | solution.py:465
  24.3 10.4 %collective-permute-start.7 = (f32[256,128]{1,0:T(8,128)S(1)}, f32[256,128]{1,0:T(8,128)S(1)}, u32[]{:S(2)}, u32[]{:S(2)}) collective-permute-start(f32[256,128]{1,0:T(8,128)S(1)} %get-tuple-element.61), channel_id=1, source_target_pairs={{0,24},{2,26},{4,28},{6,30},{8,16},{10,18},{12,20},{14,22},{16,8},... | collective-permute-start | bytes 393224 | tf_op jit(solution)/shard_map/ppermute | solution.py:465
  27.6 13.6 %collective-permute-start.9 = (f32[264,128]{1,0:T(8,128)S(1)}, f32[264,128]{1,0:T(8,128)S(1)}, u32[]{:S(2)}, u32[]{:S(2)}) collective-permute-start(f32[264,128]{1,0:T(8,128)S(1)} %get-tuple-element.70), channel_id=1, source_target_pairs={{0,4},{2,6},{4,0},{6,2},{8,12},{10,14},{12,8},{14,10},{16,20},{18,... | collective-permute-start | bytes 405512 | tf_op jit(solution)/shard_map/ppermute | solution.py:465
  31.4 9.8 %collective-permute-start.10 = (f32[264,128]{1,0:T(8,128)S(1)}, f32[264,128]{1,0:T(8,128)S(1)}, u32[]{:S(2)}, u32[]{:S(2)}) collective-permute-start(f32[264,128]{1,0:T(8,128)S(1)} %get-tuple-element.71), channel_id=1, source_target_pairs={{0,8},{2,10},{4,12},{6,14},{8,0},{10,2},{12,4},{14,6},{16,24},{18,... | collective-permute-start | bytes 405512 | tf_op jit(solution)/shard_map/ppermute | solution.py:465
  31.4 9.8 %collective-permute-start.11 = (f32[264,128]{1,0:T(8,128)S(1)}, f32[264,128]{1,0:T(8,128)S(1)}, u32[]{:S(2)}, u32[]{:S(2)}) collective-permute-start(f32[264,128]{1,0:T(8,128)S(1)} %get-tuple-element.72), channel_id=1, source_target_pairs={{0,12},{2,14},{4,8},{6,10},{8,4},{10,6},{12,0},{14,2},{16,28},{18,... | collective-permute-start | bytes 405512 | tf_op jit(solution)/shard_map/ppermute | solution.py:465
  31.4 9.8 %collective-permute-start.12 = (f32[264,128]{1,0:T(8,128)S(1)}, f32[264,128]{1,0:T(8,128)S(1)}, u32[]{:S(2)}, u32[]{:S(2)}) collective-permute-start(f32[264,128]{1,0:T(8,128)S(1)} %get-tuple-element.73), channel_id=1, source_target_pairs={{0,28},{2,30},{4,24},{6,26},{8,20},{10,22},{12,16},{14,18},{16,12}... | collective-permute-start | bytes 405512 | tf_op jit(solution)/shard_map/ppermute | solution.py:465
  34.7 6.5 %collective-permute-start.15 = (f32[8,128]{1,0:T(8,128)S(1)}, f32[8,128]{1,0:T(8,128)S(1)}, u32[]{:S(2)}, u32[]{:S(2)}) collective-permute-start(f32[8,128]{1,0:T(8,128)S(1)} %get-tuple-element.77), channel_id=1, source_target_pairs={{0,24},{2,26},{4,28},{6,30},{8,16},{10,18},{12,20},{14,22},{16,8},... | collective-permute-start | bytes 12296 | tf_op jit(solution)/shard_map/ppermute | solution.py:465
